TPU v7x, 512 devices: a whole 4x4x16 slice. The times are simulated.
512 devices in a mesh: dp: 8 (over x, y_hi), space: 64 (over y_lo, z, core).
Axes of the slice: x: 4, y: 4 (y_hi: 2, y_lo: 2; y = y_hi * 2 + y_lo), z: 16, core: 2. Of those that a mesh axis runs over, the one named last changes fastest.
Arguments:
- tiles_in: bfloat16 [8, 256, 8, 8, 384], P('dp', 'space'), may hold values from -6 to 6
- upstream: bfloat16 [8, 256, 8, 8, 384], P('dp', 'space'), may hold values from -1.1953125 to 1.1953125
- pool_weight: float32 [8, 256], P('dp', 'space'), may hold values from 0.25 to 4
- slide_cot: float32 [8, 384], P('dp'), may hold values from -6 to 6
- adjacency: int32 [8, 256, 8], P('dp', 'space'), may hold values from -1 to 255, as said below
- counts: int32 [8, 64], P('dp', 'space'), may hold values from 1 to 4, as said below
- kernel: float32 [7, 7, 384], replicated, may hold values from -0.875 to 0.875
- norm_gain: float32 [384], replicated, may hold values from 0.5 to 1.5
- w_in: bfloat16 [384, 1536], replicated, may hold values from -0.3125 to 0.3125
- w_out: bfloat16 [1536, 384], replicated, may hold values from -0.15625 to 0.15625
- layer_scale: float32 [384], replicated, may hold values from 0.1 to 1
Outputs:
- embedding: float32 [8, 384], P('dp')
- grad_tiles: bfloat16 [8, 256, 8, 8, 384], P('dp', 'space')
- grad_w_out: float32 [1536, 384], P('space')
- grad_kernel: float32 [7, 7, 384], replicated
Inputs may be any that keep to these rules, and one draw needn't show every extreme that they name: Slots form blocks of 4; block k of a slide is one row of tiles, its live tiles in its first counts slots in column order; the last block of every slide is full, and often another one too. `adjacency`: tiles lie on a grid: entries 0, 4, 5 name live slots of the block before the tile's own, entries 1, 6, 7 of the block after it, entries 2 and 3 of its own block. The lists are mutual (b is the north neighbour of a exactly when a is the south neighbour of b, and likewise for the other directions). Slots that are not live have no neighbours and are named by none.
All inputs are finite; a program needn't handle non-finite values.
Results may differ from a plain program's by a relative error of at most 0.011.
Values may be sent and summed in bfloat16 or wider, within the bound.
A program may use at most 64 MiB of HBM per device.

v0:
```python
import jax
import jax.numpy as jnp
from jax import lax
from jax.sharding import PartitionSpec as P

sqrt_half = 0.7071067811865476
inv_root_two_pi = 0.3989422804014327


def passed_along(value, axis, steps):
    count = lax.axis_size(axis)
    leading, last = (max(0, -steps), min(count, count - steps))
    return lax.ppermute(value, axis, [(source, source + steps) for source in range(leading, last)])


def depthwise(padded, kernel, tile_side):
    total = jnp.zeros(padded.shape[:1] + (tile_side, tile_side, padded.shape[3]), jnp.float32)
    for row_tap in range(7):
        for col_tap in range(7):
            window = padded[
                :, row_tap : row_tap + tile_side, col_tap : col_tap + tile_side, :
            ].astype(jnp.float32)
            total = total + window * kernel[row_tap, col_tap]
    return total


def pick(source, wanted, offset):
    valid = wanted >= 0
    index = jnp.clip(wanted - offset, 0, source.shape[0] - 1)
    chosen = jnp.take(source, index, axis=0)
    return jnp.where(valid[:, None, None, None], chosen, jnp.zeros_like(chosen))


def frame(
    own, north_rows, south_rows, right_cols, left_cols, wanted, north_base, own_base, south_base
):
    tile_side = own.shape[1]
    upper = jnp.concatenate(
        [
            pick(north_rows, wanted[:, 4], north_base)[:, :, tile_side - 3 :],
            pick(north_rows, wanted[:, 0], north_base),
            pick(north_rows, wanted[:, 5], north_base)[:, :, :3],
        ],
        axis=2,
    )
    middle = jnp.concatenate(
        [pick(right_cols, wanted[:, 2], own_base), own, pick(left_cols, wanted[:, 3], own_base)],
        axis=2,
    )
    lower = jnp.concatenate(
        [
            pick(south_rows, wanted[:, 6], south_base)[:, :, tile_side - 3 :],
            pick(south_rows, wanted[:, 1], south_base),
            pick(south_rows, wanted[:, 7], south_base)[:, :, :3],
        ],
        axis=2,
    )
    return jnp.concatenate([upper, middle, lower], axis=1)


def block_pass(
    padded, own, upstream, pool_weight, live, slide_cot, kernel, norm_gain, w_in, w_out, layer_scale
):
    tile_side = own.shape[1]
    channels = own.shape[3]
    conv_out = depthwise(padded, kernel, tile_side)
    centred = conv_out - jnp.mean(conv_out, axis=-1, keepdims=True)
    inv_std = lax.rsqrt(jnp.mean(centred * centred, axis=-1, keepdims=True) + 1e-06)
    normed = centred * inv_std
    lifted = (normed * norm_gain).astype(jnp.bfloat16).reshape(-1, channels)
    pre = jnp.dot(lifted, w_in, preferred_element_type=jnp.float32)
    cdf = 0.5 * (1.0 + jax.scipy.special.erf(pre * sqrt_half))
    activated = (pre * cdf).astype(jnp.bfloat16)
    mixed = jnp.dot(activated, w_out, preferred_element_type=jnp.float32).reshape(own.shape)
    block_out = own.astype(jnp.float32) + layer_scale * mixed
    weight_live = live * pool_weight
    emb_term = jnp.sum(weight_live[:, None] * jnp.sum(block_out, axis=(1, 2)), axis=0) / tile_side
    extra = pool_weight[:, None] * slide_cot[None, :] / tile_side
    grad_out = live[:, None, None, None] * (upstream.astype(jnp.float32) + extra[:, None, None, :])
    grad_mixed = (grad_out * layer_scale).astype(jnp.bfloat16).reshape(-1, channels)
    grad_act = lax.dot_general(
        grad_mixed, w_out, (((1,), (1,)), ((), ())), preferred_element_type=jnp.float32
    )
    density = jnp.exp(-0.5 * pre * pre) * inv_root_two_pi
    grad_pre = (grad_act * (cdf + pre * density)).astype(jnp.bfloat16)
    grad_lift = lax.dot_general(
        grad_pre, w_in, (((1,), (1,)), ((), ())), preferred_element_type=jnp.float32
    )
    grad_normed = grad_lift.reshape(own.shape) * norm_gain
    grad_conv = inv_std * (
        grad_normed
        - jnp.mean(grad_normed, axis=-1, keepdims=True)
        - normed * jnp.mean(grad_normed * normed, axis=-1, keepdims=True)
    )
    kernel_rows = []
    for row_tap in range(7):
        for col_tap in range(7):
            window = padded[
                :, row_tap : row_tap + tile_side, col_tap : col_tap + tile_side, :
            ].astype(jnp.float32)
            kernel_rows.append(jnp.sum(window * grad_conv, axis=(0, 1, 2)))
    kernel_grad = jnp.stack(kernel_rows).reshape(7, 7, channels)
    return (emb_term, grad_out, grad_conv, activated, grad_mixed, kernel_grad)


def per_device(
    tiles_in,
    upstream,
    pool_weight,
    slide_cot,
    adjacency,
    counts,
    kernel,
    norm_gain,
    w_in,
    w_out,
    layer_scale,
):
    own = tiles_in[0]
    capacity = own.shape[0]
    tile_side = own.shape[1]
    position = lax.axis_index("space")
    own_base = position * capacity
    north_base = own_base - capacity
    south_base = own_base + capacity
    wanted = adjacency[0]
    live = (jnp.arange(capacity, dtype=jnp.int32) < counts[0, 0]).astype(jnp.float32)
    north_rows = passed_along(own[:, tile_side - 3 :], "space", 1)
    south_rows = passed_along(own[:, :3], "space", -1)
    padded = frame(
        own,
        north_rows,
        south_rows,
        own[:, :, tile_side - 3 :],
        own[:, :, :3],
        wanted,
        north_base,
        own_base,
        south_base,
    )
    emb_term, grad_out, grad_conv, activated, grad_mixed, kernel_grad = block_pass(
        padded,
        own,
        upstream[0],
        pool_weight[0],
        live,
        slide_cot[0],
        kernel,
        norm_gain,
        w_in,
        w_out,
        layer_scale,
    )
    embedding = lax.psum(emb_term, "space")
    local_weight = lax.dot_general(
        activated, grad_mixed, (((0,), (0,)), ((), ())), preferred_element_type=jnp.float32
    )
    whole_weight, kernel_dp = (
        lax.psum(local_weight.astype(jnp.bfloat16), "dp").astype(jnp.float32),
        lax.psum(kernel_grad.astype(jnp.bfloat16), "dp").astype(jnp.float32),
    )
    weight_share = lax.psum_scatter(whole_weight, "space", scatter_dimension=0, tiled=True)
    kernel_total = lax.psum(kernel_dp, "space")
    grad_north = passed_along(
        grad_conv[:, tile_side - 3 :].astype(jnp.bfloat16), "space", 1
    ).astype(jnp.float32)
    grad_south = passed_along(grad_conv[:, :3].astype(jnp.bfloat16), "space", -1).astype(
        jnp.float32
    )
    padded_grad = frame(
        grad_conv,
        grad_north,
        grad_south,
        grad_conv[:, :, tile_side - 3 :],
        grad_conv[:, :, :3],
        wanted,
        north_base,
        own_base,
        south_base,
    )
    back = depthwise(padded_grad, kernel[::-1, ::-1], tile_side)
    grad_tiles = ((grad_out + back) * live[:, None, None, None]).astype(jnp.bfloat16)
    return (embedding[None, :], grad_tiles[None], weight_share, kernel_total)


def solution(mesh):
    return jax.shard_map(
        per_device,
        mesh=mesh,
        in_specs=(
            P("dp", "space", None, None, None),
            P("dp", "space", None, None, None),
            P("dp", "space"),
            P("dp", None),
            P("dp", "space", None),
            P("dp", "space"),
            P(),
            P(),
            P(),
            P(),
            P(),
        ),
        out_specs=(P("dp", None), P("dp", "space", None, None, None), P("space", None), P()),
        check_vma=False,
    )
```

profile of v0, /device:TPU:24, one launch (start us, length us, event | category | flops | bytes accessed | tf_op | source)
XLA Modules:
  0.0 443.2 jit_solution(4446253481833367217)
XLA Ops:
  7.2 1.0 fusion.191
  8.3 1.9 collective-permute-start
  10.2 11.0 %collective-permute-start.1 = (bf16[4,3,8,384]{3,2,1,0:T(8,128)(2,1)S(1)}, bf16[4,3,8,384]{3,2,1,0:T(8,128)(2,1)S(1)}, u32[]{:S(2)}, u32[]{:S(2)}) collective-permute-start(bf16[4,3,8,384]{3,2,1,0:T(8,128)(2,1)S(1)} %get-tuple-element.147), channel_id=1, source_target_pairs={{1,0},{2,1},{3,2},{4,3},{5,4},{6,5},{7,6},{8,7},{9,8},{10,9},{11,1... | collective-permute-start | bytes 221192 | tf_op jit(solution)/shard_map/ppermute | solution.py:13
  21.2 1.1 fusion.192
  22.4 1.3 compare_reduce_fusion.7
  23.7 1.3 clamp_reduce_fusion.7
  26.7 1.0 slice_reduce_fusion.46
  27.8 1.8 slice_reduce_fusion.48
  29.7 1.9 slice_reduce_fusion.47
  35.5 0.8 select_select_fusion.4
  36.3 0.8 select_select_fusion.5
  37.8 0.8 fusion.182
  44.0 4.2 fusion.187
  48.7 1.7 multiply_convert_fusion
  50.4 0.9 copy-done.1
  51.3 1.6 convolution_convert_fusion
  53.6 3.1 multiply_reduce_fusion.1
  57.1 96.8 %all-reduce.5.cloned.1.call-done = bf16[1536,384]{1,0:T(8,128)(2,1)} async-done(((bf16[1536,384]{1,0:T(8,128)(2,1)}), bf16[1536,384]{1,0:T(8,128)(2,1)}) %all-reduce.5.cloned.1.call-update) | async-done | bytes 1179664 | tf_op jit(solution)/shard_map/psum | solution.py:159
  153.9 2.8 convert_element_type.315
  156.8 2.0 fusion.186
  158.7 3.2 fusion.85
  162.0 0.9 gather_fusion.12
  162.9 0.8 gather_fusion.11
  164.4 1.9 collective-permute-start.2
  166.3 5.9 %collective-permute-start.3 = (bf16[4,3,8,384]{3,2,1,0:T(8,128)(2,1)S(1)}, bf16[4,3,8,384]{3,2,1,0:T(8,128)(2,1)S(1)}, u32[]{:S(2)}, u32[]{:S(2)}) collective-permute-start(bf16[4,3,8,384]{3,2,1,0:T(8,128)(2,1)S(1)} %get-tuple-element.145), channel_id=1, source_target_pairs={{1,0},{2,1},{3,2},{4,3},{5,4},{6,5},{7,6},{8,7},{9,8},{10,9},{11,1... | collective-permute-start | bytes 221192 | tf_op jit(solution)/shard_map/ppermute | solution.py:13
  172.2 0.8 multiply_reduce_fusion.3
  173.7 0.8 select_select_fusion.1
  174.5 1.0 fusion.53
  175.6 1.0 fusion.103
  177.7 38.1 %psum.30 = bf16[7,7,384]{2,1,0:T(8,128)(2,1)S(1)} all-reduce(bf16[7,7,384]{2,1,0:T(8,128)(2,1)S(1)} %convert_element_type.316), channel_id=1, replica_groups=mesh['dp'=8,'space'=64] {'dp'}, use_global_device_ids=true, to_apply=%region_58.63 | all-reduce | flops 18816 | bytes 75264 | tf_op jit(solution)/shard_map/psum | solution.py:160
  215.8 208.1 %all-reduce.6 = (f32[1,384]{1,0:T(1,128)}, f32[7,7,384]{2,1,0:T(8,128)}) all-reduce(f32[1,384]{1,0:T(1,128)S(1)} %broadcast_in_dim.154, bf16[7,7,384]{2,1,0:T(8,128)(2,1)S(1)} %psum.30), channel_id=1, replica_groups=mesh['dp'=8,'space'=64] {'space'}, use_global_device_ids=true, to_apply=%region_4.7 | all-reduce | flops 19200 | bytes 115968 | tf_op jit(solution)/shard_map/psum | solution.py:154
  432.0 4.4 %fusion.175 = bf16[1,4,8,8,384]{4,3,2,1,0:T(8,128)(2,1)} fusion(f32[384]{0:T(512)S(1)} %copy-done.21, f32[4,11,14,384]{3,2,1,0:T(8,128)S(1)} %get-tuple-element.139, f32[384]{0:T(512)S(1)} %copy-done.56, f32[384]{0:T(512)S(1)} %get-tuple-element.105, f32[384]{0:T(512)S(1)} %copy-done.15, f32[384]{0:T(512)S(1)} %copy-done.13, f32[384]{0:T(512)S(1)} %copy-done.11, ...), kind=kLoop, calls=%fused_computation.371 | loop fusion | flops 10715136 | bytes 17677840 | tf_op jit(solution)/shard_map/broadcast_in_dim | solution.py:183
  (352 shorter events, 21.4 us)
Async XLA Ops:
  7.2 41.5 %copy-start = (bf16[384,1536]{1,0:T(8,128)(2,1)S(1)}, bf16[384,1536]{1,0:T(8,128)(2,1)}, u32[]{:S(2)}) copy-start(bf16[384,1536]{1,0:T(8,128)(2,1)} %param.27) | copy-start | bytes 3538948
  7.2 29.9 %copy-start.71 = (f32[384]{0:T(512)S(1)}, f32[384]{0:T(512)}, u32[]{:S(2)}) copy-start(f32[384]{0:T(512)} %param.29) | copy-start | bytes 4612
  7.2 29.9 %copy-start.5 = (bf16[1,4,8,8,384]{4,3,2,1,0:T(8,128)(2,1)S(1)}, bf16[1,4,8,8,384]{4,3,2,1,0:T(8,128)(2,1)}, u32[]{:S(2)}) copy-start(bf16[1,4,8,8,384]{4,3,2,1,0:T(8,128)(2,1)} %param.20) | copy-start | bytes 589828
  7.2 146.7 %all-reduce.5.cloned.1.call-start = ((), (), s32[]{:S(2)}) async-start(), calls=%async_computation.1 | async-start | bytes 2359296 | tf_op jit(solution)/shard_map/psum | solution.py:159
  8.3 29.0 %collective-permute-start = (bf16[4,3,8,384]{3,2,1,0:T(8,128)(2,1)S(1)}, bf16[4,3,8,384]{3,2,1,0:T(8,128)(2,1)S(1)}, u32[]{:S(2)}, u32[]{:S(2)}) collective-permute-start(bf16[4,3,8,384]{3,2,1,0:T(8,128)(2,1)S(1)} %get-tuple-element.146), channel_id=1, source_target_pairs={{0,1},{1,2},{2,3},{3,4},{4,5},{5,6},{6,7},{7,8},{8,9},{9,10},{10,1... | collective-permute-start | bytes 221192 | tf_op jit(solution)/shard_map/ppermute | solution.py:13
  10.2 30.3 %collective-permute-start.1 = (bf16[4,3,8,384]{3,2,1,0:T(8,128)(2,1)S(1)}, bf16[4,3,8,384]{3,2,1,0:T(8,128)(2,1)S(1)}, u32[]{:S(2)}, u32[]{:S(2)}) collective-permute-start(bf16[4,3,8,384]{3,2,1,0:T(8,128)(2,1)S(1)} %get-tuple-element.147), channel_id=1, source_target_pairs={{1,0},{2,1},{3,2},{4,3},{5,4},{6,5},{7,6},{8,7},{9,8},{10,9},{11,1... | collective-permute-start | bytes 221192 | tf_op jit(solution)/shard_map/ppermute | solution.py:13
  23.6 17.5 %copy-start.83 = (pred[4]{0:T(512)(128)(4,1)}, pred[4]{0:T(512)(128)(4,1)S(1)}, u32[]{:S(2)}) copy-start(pred[4]{0:T(512)(128)(4,1)S(1)} %get-tuple-element.123) | copy-start | bytes 16
  23.6 17.5 %copy-start.89 = (pred[4]{0:T(512)(128)(4,1)}, pred[4]{0:T(512)(128)(4,1)S(1)}, u32[]{:S(2)}) copy-start(pred[4]{0:T(512)(128)(4,1)S(1)} %get-tuple-element.116) | copy-start | bytes 16
  23.7 17.5 %copy-start.91 = (pred[4]{0:T(512)(128)(4,1)}, pred[4]{0:T(512)(128)(4,1)S(1)}, u32[]{:S(2)}) copy-start(pred[4]{0:T(512)(128)(4,1)S(1)} %get-tuple-element.122) | copy-start | bytes 16
  23.7 17.5 %copy-start.93 = (pred[4]{0:T(512)(128)(4,1)}, pred[4]{0:T(512)(128)(4,1)S(1)}, u32[]{:S(2)}) copy-start(pred[4]{0:T(512)(128)(4,1)S(1)} %get-tuple-element.121) | copy-start | bytes 16
  23.7 17.5 %copy-start.94 = (pred[4]{0:T(512)(128)(4,1)}, pred[4]{0:T(512)(128)(4,1)S(1)}, u32[]{:S(2)}) copy-start(pred[4]{0:T(512)(128)(4,1)S(1)} %get-tuple-element.120) | copy-start | bytes 16
  23.7 17.5 %copy-start.87 = (pred[4]{0:T(512)(128)(4,1)}, pred[4]{0:T(512)(128)(4,1)S(1)}, u32[]{:S(2)}) copy-start(pred[4]{0:T(512)(128)(4,1)S(1)} %get-tuple-element.117) | copy-start | bytes 16
  23.7 18.3 %copy-start.81 = (pred[4]{0:T(512)(128)(4,1)}, pred[4]{0:T(512)(128)(4,1)S(1)}, u32[]{:S(2)}) copy-start(pred[4]{0:T(512)(128)(4,1)S(1)} %get-tuple-element.118) | copy-start | bytes 16
  23.7 18.9 %copy-start.85 = (pred[4]{0:T(512)(128)(4,1)}, pred[4]{0:T(512)(128)(4,1)S(1)}, u32[]{:S(2)}) copy-start(pred[4]{0:T(512)(128)(4,1)S(1)} %get-tuple-element.119) | copy-start | bytes 16
  25.0 16.2 %copy-start.99 = (pred[4]{0:T(512)(128)(4,1)}, pred[4]{0:T(512)(128)(4,1)S(1)}, u32[]{:S(2)}) copy-start(pred[4]{0:T(512)(128)(4,1)S(1)} %get-tuple-element.160) | copy-start | bytes 16
  25.0 16.9 %copy-start.95 = (pred[4]{0:T(512)(128)(4,1)}, pred[4]{0:T(512)(128)(4,1)S(1)}, u32[]{:S(2)}) copy-start(pred[4]{0:T(512)(128)(4,1)S(1)} %get-tuple-element.161) | copy-start | bytes 16
  25.6 15.6 %copy-start.97 = (pred[4]{0:T(512)(128)(4,1)}, pred[4]{0:T(512)(128)(4,1)S(1)}, u32[]{:S(2)}) copy-start(pred[4]{0:T(512)(128)(4,1)S(1)} %get-tuple-element.166) | copy-start | bytes 16
  27.7 16.1 %copy-start.10 = (f32[384]{0:T(512)}, f32[384]{0:T(512)S(1)}, u32[]{:S(2)}) copy-start(f32[384]{0:T(512)S(1)} %get-tuple-element.111) | copy-start | bytes 4612
  27.7 16.1 %copy-start.12 = (f32[384]{0:T(512)}, f32[384]{0:T(512)S(1)}, u32[]{:S(2)}) copy-start(f32[384]{0:T(512)S(1)} %get-tuple-element.112) | copy-start | bytes 4612
  27.7 16.1 %copy-start.14 = (f32[384]{0:T(512)}, f32[384]{0:T(512)S(1)}, u32[]{:S(2)}) copy-start(f32[384]{0:T(512)S(1)} %get-tuple-element.113) | copy-start | bytes 4612
  27.7 16.1 %copy-start.16 = (f32[384]{0:T(512)}, f32[384]{0:T(512)S(1)}, u32[]{:S(2)}) copy-start(f32[384]{0:T(512)S(1)} %get-tuple-element.114) | copy-start | bytes 4612
  27.8 16.1 %copy-start.18 = (f32[384]{0:T(512)}, f32[384]{0:T(512)S(1)}, u32[]{:S(2)}) copy-start(f32[384]{0:T(512)S(1)} %get-tuple-element.115) | copy-start | bytes 4612
  29.6 14.3 %copy-start.30 = (f32[384]{0:T(512)}, f32[384]{0:T(512)S(1)}, u32[]{:S(2)}) copy-start(f32[384]{0:T(512)S(1)} %get-tuple-element.72) | copy-start | bytes 4612
  29.6 14.3 %copy-start.32 = (f32[384]{0:T(512)}, f32[384]{0:T(512)S(1)}, u32[]{:S(2)}) copy-start(f32[384]{0:T(512)S(1)} %get-tuple-element.73) | copy-start | bytes 4612
  29.6 14.3 %copy-start.34 = (f32[384]{0:T(512)}, f32[384]{0:T(512)S(1)}, u32[]{:S(2)}) copy-start(f32[384]{0:T(512)S(1)} %get-tuple-element.74) | copy-start | bytes 4612
  29.6 14.3 %copy-start.36 = (f32[384]{0:T(512)}, f32[384]{0:T(512)S(1)}, u32[]{:S(2)}) copy-start(f32[384]{0:T(512)S(1)} %get-tuple-element.75) | copy-start | bytes 4612
  29.6 14.3 %copy-start.38 = (f32[384]{0:T(512)}, f32[384]{0:T(512)S(1)}, u32[]{:S(2)}) copy-start(f32[384]{0:T(512)S(1)} %get-tuple-element.76) | copy-start | bytes 4612
  52.9 383.5 %reduce-scatter.5.cloned.1.call-start = ((), (), s32[]{:S(2)}) async-start(), calls=%async_computation.2 | async-start | bytes 2396160
  56.7 100.0 %copy-start.4 = (f32[256,384]{1,0:T(8,128)}, f32[256,384]{1,0:T(8,128)S(1)}, u32[]{:S(2)}) copy-start(f32[256,384]{1,0:T(8,128)S(1)} %get-tuple-element.151) | copy-start | bytes 1179652
  164.4 259.6 %collective-permute-start.2 = (bf16[4,3,8,384]{3,2,1,0:T(8,128)(2,1)}, bf16[4,3,8,384]{3,2,1,0:T(8,128)(2,1)S(1)}, u32[]{:S(2)}, u32[]{:S(2)}) collective-permute-start(bf16[4,3,8,384]{3,2,1,0:T(8,128)(2,1)} %get-tuple-element.144), channel_id=1, source_target_pairs={{0,1},{1,2},{2,3},{3,4},{4,5},{5,6},{6,7},{7,8},{8,9},{9,10},{10,1... | collective-permute-start | bytes 221192 | tf_op jit(solution)/shard_map/ppermute | solution.py:13
  166.3 259.8 %collective-permute-start.3 = (bf16[4,3,8,384]{3,2,1,0:T(8,128)(2,1)S(1)}, bf16[4,3,8,384]{3,2,1,0:T(8,128)(2,1)S(1)}, u32[]{:S(2)}, u32[]{:S(2)}) collective-permute-start(bf16[4,3,8,384]{3,2,1,0:T(8,128)(2,1)S(1)} %get-tuple-element.145), channel_id=1, source_target_pairs={{1,0},{2,1},{3,2},{4,3},{5,4},{6,5},{7,6},{8,7},{9,8},{10,9},{11,1... | collective-permute-start | bytes 221192 | tf_op jit(solution)/shard_map/ppermute | solution.py:13
  177.7 250.4 %copy-start.92 = (pred[4]{0:T(512)(128)(4,1)S(1)}, pred[4]{0:T(512)(128)(4,1)}, u32[]{:S(2)}) copy-start(pred[4]{0:T(512)(128)(4,1)} %copy-done.91) | copy-start | bytes 16
  (87 other events, 334.2 us)
Sparse Core Ops, SparseCore 0:
  53.0 100.7 all-reduce.4
  157.3 229.0 reduce-scatter.4
where the time goes:
time: 447 us; the launch traced here: 443 us
  blocking collectives  246 us (55%)
  waiting for transfers between devices  96.9 us (22%)
  other arithmetic  31.9 us (7%)
  starting transfers between devices  20.9 us (5%)
  local copies, waits for them, and re-layouts  20.7 us (5%)
  between operations  17.1 us (4%)
  matrix products  9.62 us (2%)
    psum x1, blocking collectives, per_device(): embedding = lax.psum(emb_term, 'space')  208 us
    psum x1, waiting for transfers between devices, per_device(): lax.psum(local_weight.astype(jnp.bfloat16), 'dp').astype(jnp.float32)  96.8 us
    psum x1, blocking collectives, per_device(): lax.psum(kernel_grad.astype(jnp.bfloat16), 'dp').astype(jnp.float32)  38.1 us
    ppermute x4, starting transfers between devices, passed_along(): lax.ppermute(value, axis, [(source, source + steps) for source in range(l...  20.8 us
    gather x16, local copies, waits for them, and re-layouts, pick(): chosen = jnp.take(source, index, axis=0)  10.5 us
  transfers between devices with their start and end apart: 6, of which 1 were waited for; matrix products, arithmetic and copies ran while one was open for 10% of the time, Pallas kernels for 0%

commit v1 on v0

v1 whole, which is shorter than its diff:
```python
import functools

import jax
import jax.numpy as jnp
from jax import lax
from jax.experimental import pallas as pl
from jax.experimental.pallas import tpu as pltpu
from jax.sharding import PartitionSpec as P

MESH = pl.DeviceIdType.MESH
F32, BF16 = jnp.float32, jnp.bfloat16
sqrt_half = 0.7071067811865476
inv_root_two_pi = 0.3989422804014327

C, HID, CAP, TILE = 384, 1536, 4, 8
CG = C // 128
PIX = CAP * TILE * TILE
CHUNK = 384
ROWS = 52


def spread(adj, t, pad, own, north, south):
    def entry(e):
        wanted = adj[t, e]
        return jnp.bitwise_and(jnp.maximum(wanted, 0), CAP - 1), wanted >= 0

    parts = (
        (3, 8, (own, 2), (own, None), (own, 3)),
        (0, 3, (north, 4), (north, 0), (north, 5)),
        (11, 3, (south, 6), (south, 1), (south, 7)),
    )
    for row, rows, *columns in parts:
        for place, (source, e) in enumerate(columns):
            if e is None:
                groups = source(t)
            else:
                index, valid = entry(e)
                groups = [jnp.where(valid, g, 0.0) for g in source(index)]
            for g in range(CG):
                pad[g, t, row : row + rows, 8 * place : 8 * place + 8, :] = groups[g]


def conv_tile(pad, taps, g, t, flip):
    total = [None] * TILE
    for j in range(7):
        column = [taps[g, 48 - (i * 7 + j) if flip else i * 7 + j] for i in range(7)]
        for r in range(14):
            window = pad[g, t, r, 5 + j : 13 + j, :]
            for i in range(7):
                a = r - i
                if 0 <= a < TILE:
                    term = window * column[i]
                    total[a] = term if total[a] is None else total[a] + term
    return total


def split_groups(value):
    return [value[..., g * 128 : (g + 1) * 128] for g in range(CG)]


def live_of(cnt, t):
    return jnp.where(t < cnt[0, 0], 1.0, 0.0).astype(F32)


def grad_out_of(up, pw, cot, live, t):
    extra = pw[0, t] * cot[...] / TILE
    return live * (up[t].astype(F32) + extra[None])


def load_taps(ker, taps):
    for ij in range(49):
        row = ker[ij // 7, ij % 7 : ij % 7 + 1, :]
        for g in range(CG):
            taps[g, ij] = jnp.broadcast_to(row[:, g * 128 : (g + 1) * 128], (8, 128))


def forward_backward(
    pw, adj, cnt, own, north, south, up, cot, ker, gain, scale, w_in_hbm, w_out_hbm,
    grads, emb, gconv, edge_first, edge_last,
    pad, taps, normed, inv, lifted, gmix, glift, w_in, w_out, sems,
):
    loads = [
        pltpu.make_async_copy(w_in_hbm, w_in, sems.at[0]),
        pltpu.make_async_copy(w_out_hbm, w_out, sems.at[1]),
    ]
    for load in loads:
        load.start()
    load_taps(ker, taps)

    def groups_of(ref):
        return lambda i: split_groups(ref[i].astype(F32))

    @pl.loop(0, CAP)
    def _(t):
        spread(adj, t, pad, groups_of(own), groups_of(north), groups_of(south))

    @pl.loop(0, CAP)
    def _(t):
        @pl.loop(0, CG)
        def _(g):
            rows = conv_tile(pad, taps, g, t, False)
            for a in range(TILE):
                normed[g, t, a] = rows[a]

    emb_own = jnp.zeros((1, C), F32)
    for t in range(CAP):
        live = live_of(cnt, t)
        x = [normed[g, t].reshape(64, 128) for g in range(CG)]
        mean = jnp.sum(x[0] + x[1] + x[2], axis=-1, keepdims=True) / C
        x = [v - mean for v in x]
        var = jnp.sum(x[0] * x[0] + x[1] * x[1] + x[2] * x[2], axis=-1, keepdims=True) / C
        istd = jnp.broadcast_to(lax.rsqrt(var + 1e-06), (64, 128))
        inv[t] = istd
        here = slice(t * 64, t * 64 + 64)
        for g in range(CG):
            lanes = slice(g * 128, g * 128 + 128)
            n = x[g] * istd
            normed[g, t] = n.reshape(TILE, TILE, 128)
            lifted[here, lanes] = (n * gain[:, lanes]).astype(BF16)
        g_out = grad_out_of(up, pw, cot, live, t)
        gmix[here, :] = (g_out * scale[...][None]).astype(BF16).reshape(64, C)
        weight = live * pw[0, t]
        emb_own = emb_own + weight * jnp.sum(own[t].astype(F32).reshape(64, C), axis=0, keepdims=True)

    for load in loads:
        load.wait()
    mixed = jnp.zeros((8, C), F32)
    for h in range(HID // CHUNK):
        here = slice(h * CHUNK, (h + 1) * CHUNK)
        pre = jnp.dot(lifted[...], w_in[:, here], preferred_element_type=F32)
        cdf = 0.5 * (1.0 + lax.erf(pre * sqrt_half))
        act = (pre * cdf).astype(BF16)
        gact = lax.dot_general(
            gmix[...], w_out[here, :], (((1,), (1,)), ((), ())), preferred_element_type=F32
        )
        density = jnp.exp(-0.5 * pre * pre) * inv_root_two_pi
        gpre = (gact * (cdf + pre * density)).astype(BF16)
        gl = lax.dot_general(
            gpre, w_in[:, here], (((1,), (1,)), ((), ())), preferred_element_type=F32
        )
        if h == 0:
            glift[...] = gl
        else:
            glift[...] += gl
        pooled = jnp.zeros((1, CHUNK), F32)
        for t in range(CAP):
            weight = live_of(cnt, t) * pw[0, t]
            pooled = pooled + weight * jnp.sum(
                act[t * 64 : t * 64 + 64].astype(F32), axis=0, keepdims=True
            )
        high = pooled.astype(BF16)
        rest = pooled - high.astype(F32)
        middle = rest.astype(BF16)
        low = (rest - middle.astype(F32)).astype(BF16)
        three = jnp.concatenate([high, middle, low, jnp.zeros((5, CHUNK), BF16)], axis=0)
        mixed = mixed + jnp.dot(three, w_out[here, :], preferred_element_type=F32)
        gw = lax.dot_general(
            act, gmix[...], (((0,), (0,)), ((), ())), preferred_element_type=F32
        ).astype(BF16)
        for q in range(CHUNK // 24):
            block = h * (CHUNK // 24) + q
            core, plane, z = block % 2, block // 32, block // 2 % 16
            chunk, row = z // 2 * 2 + plane, z % 2 * 24
            grads[core, chunk, row : row + 24, :] = gw[q * 24 : q * 24 + 24, :]
    mix = jnp.sum(mixed, axis=0, keepdims=True)
    emb[...] = jnp.broadcast_to((emb_own + scale[...] * mix) / TILE, (8, C))

    for t in range(CAP):
        here = slice(t * 64, t * 64 + 64)
        gn = [glift[here, g * 128 : g * 128 + 128] * gain[:, g * 128 : g * 128 + 128] for g in range(CG)]
        n = [normed[g, t].reshape(64, 128) for g in range(CG)]
        m1 = jnp.sum(gn[0] + gn[1] + gn[2], axis=-1, keepdims=True) / C
        m2 = jnp.sum(gn[0] * n[0] + gn[1] * n[1] + gn[2] * n[2], axis=-1, keepdims=True) / C
        for g in range(CG):
            gc = (inv[t] * (gn[g] - m1 - n[g] * m2)).reshape(TILE, TILE, 128)
            gconv[g, t] = gc
            edge_first[g, t] = gc[:3].astype(BF16)
            edge_last[g, t] = gc[TILE - 3 :].astype(BF16)

    for g in range(CG):
        lanes = slice(g * 128, g * 128 + 128)
        for j in range(7):

            def tile_taps(t, carry, j=j, g=g):
                gc = [gconv[g, t, a] for a in range(TILE)]
                out = list(carry)
                for r in range(14):
                    window = pad[g, t, r, 5 + j : 13 + j, :]
                    for i in range(7):
                        a = r - i
                        if 0 <= a < TILE:
                            out[i] = out[i] + window * gc[a]
                return tuple(out)

            sums = lax.fori_loop(
                0, CAP, tile_taps, tuple(jnp.zeros((8, 128), F32) for _ in range(7))
            )
            for i in range(7):
                taps[g, i * 7 + j] = sums[i]
        total = jnp.sum(taps[g], axis=1)
        total = jnp.concatenate([total, jnp.zeros((15, 128), F32)], axis=0)
        for chunk in range(16):
            part = total[chunk * 4 : chunk * 4 + 4].astype(BF16)
            for core in range(2):
                grads[core, chunk, 48:52, lanes] = part


def reduce_kernel(
    spaces, first, last, grads, emb,
    north_out, south_out, w_out, k_out, emb_out,
    got1, emb1, send2, got2, emb_sum, emb2, send3, got3, send4w, send4k, half, other,
    s_halo, r_halo, s1, r1, s2, r2, s_e, r_e, s3, r3, s4w, r4w, s4k, r4k, s5, r5,
):
    dp, space = lax.axis_index("dp"), lax.axis_index("space")
    core = lax.rem(space, 2)
    z = lax.rem(space // 2, 16)
    plane = space // 32
    spot = dp * 2 + plane

    def at(d, p, zz, c):
        return (d, (p * 16 + zz) * 2 + c)

    def chunk_device(q):
        return at(q // 2, lax.rem(q, 2), z, core)

    partner = at(dp, plane, z, 1 - core)
    before = (dp, lax.rem(space + spaces - 1, spaces))
    after = (dp, lax.rem(space + 1, spaces))
    home_z = 2 * dp + z // 8

    barrier = pltpu.get_barrier_semaphore()

    def greet(device):
        pl.semaphore_signal(barrier, inc=1, device_id=device, device_id_type=MESH)

    greet(partner)
    greet(before)
    greet(after)

    @pl.loop(1, 16)
    def _(k):
        greet(chunk_device(lax.rem(spot + k, 16)))
        greet(at(dp, plane, lax.rem(z + k, 16), core))

    own_home = home_z == z

    @pl.loop(0, 8)
    def _(k):
        mine = jnp.logical_and(own_home, k == lax.rem(z, 8))

        @pl.when(jnp.logical_not(mine))
        def _():
            greet(at(z // 2, plane, 8 * lax.rem(z, 2) + k, core))

    @pl.when(own_home)
    def _():
        pl.semaphore_wait(barrier, 3 + 30 + 7)

    @pl.when(jnp.logical_not(own_home))
    def _():
        pl.semaphore_wait(barrier, 3 + 30 + 8)

    def copy(src, dst, send, recv, device):
        return pltpu.make_async_remote_copy(
            src_ref=src, dst_ref=dst, send_sem=send, recv_sem=recv,
            device_id=device, device_id_type=MESH,
        )

    pair = copy(grads.at[1 - core], got1, s1.at[0], r1.at[0], partner)
    pair_emb = copy(emb, emb1, s1.at[1], r1.at[1], partner)
    pair.start()
    pair_emb.start()
    to_after = copy(last, north_out, s_halo.at[0], r_halo.at[0], after)
    to_before = copy(first, south_out, s_halo.at[1], r_halo.at[1], before)
    to_after.start()
    to_before.start()
    pair_emb.wait()
    emb_sum[...] = emb[...] + emb1[...]
    across = copy(emb_sum, emb2, s_e.at[0], r_e.at[0], at(dp, 1 - plane, z, core))
    across.start()
    pair.wait()

    def sum2(q):
        send2[q] = (grads[core, q].astype(F32) + got1[q].astype(F32)).astype(BF16)

    @pl.loop(1, 16)
    def _(k):
        q = lax.rem(spot + k, 16)
        sum2(q)
        copy(send2.at[q], got2.at[spot], s2.at[k], r2.at[spot], chunk_device(q)).start()

    sum2(spot)
    got2[spot] = send2[spot]
    across.wait()
    emb_both = emb_sum[0:1] + emb2[0:1]
    high = emb_both.astype(BF16)
    low = emb_both - high.astype(F32)
    mine = jnp.where(core == 0, high.astype(F32), low)

    @pl.loop(1, 16)
    def _(k):
        q = lax.rem(spot + k, 16)
        copy(send2.at[q], got2.at[q], s2.at[k], r2.at[q], chunk_device(q)).wait()

    total = got2[0].astype(F32)
    for q in range(1, 16):
        total = total + got2[q].astype(F32)

    tail = total[48:52]
    for q in range(16):
        send3[q] = jnp.concatenate([total[q * 3 : q * 3 + 3], tail, mine], axis=0).astype(BF16)

    @pl.loop(1, 16)
    def _(k):
        q = lax.rem(z + k, 16)
        copy(send3.at[q], got3.at[z], s3.at[k], r3.at[z], at(dp, plane, q, core)).start()

    got3[z] = send3[z]

    @pl.loop(1, 16)
    def _(k):
        q = lax.rem(z + k, 16)
        copy(send3.at[q], got3.at[q], s3.at[k], r3.at[q], at(dp, plane, q, core)).wait()

    total = got3[0].astype(F32)
    for q in range(1, 16):
        total = total + got3[q].astype(F32)

    send4w[...] = total[0:3].astype(BF16)
    send4k[...] = total[3:7].astype(BF16)
    half[...] = jnp.broadcast_to(total[7:8], (8, C))
    swap = copy(half, other, s5.at[0], r5.at[0], partner)
    swap.start()

    @pl.loop(0, 8)
    def _(d):
        mine = jnp.logical_and(own_home, d == dp)

        @pl.when(jnp.logical_not(mine))
        def _():
            copy(
                send4w, w_out.at[lax.rem(z, 8)], s4w.at[d], r4w.at[lax.rem(z, 8)],
                at(d, plane, home_z, core),
            ).start()

        @pl.when(mine)
        def _():
            w_out[lax.rem(z, 8)] = send4w[...]

    @pl.loop(1, 16)
    def _(k):
        q = lax.rem(spot + k, 16)
        copy(send4k, k_out.at[spot], s4k.at[k], r4k.at[spot], chunk_device(q)).start()

    k_out[spot] = send4k[...]
    swap.wait()
    emb_out[...] = half[...] + other[...]

    @pl.loop(0, 8)
    def _(k):
        mine = jnp.logical_and(own_home, k == lax.rem(z, 8))
        sent = jnp.logical_and(own_home, k == dp)

        @pl.when(jnp.logical_not(mine))
        def _():
            copy(send4w, w_out.at[k], s4w.at[k], r4w.at[k], partner).wait_recv()

        @pl.when(jnp.logical_not(sent))
        def _():
            copy(send4w, w_out.at[k], s4w.at[k], r4w.at[k], partner).wait_send()

    @pl.loop(1, 16)
    def _(k):
        q = lax.rem(spot + k, 16)
        copy(send4k, k_out.at[q], s4k.at[k], r4k.at[q], chunk_device(q)).wait()

    to_after.wait()
    to_before.wait()


def back_kernel(
    pw, adj, cnt, up, cot, ker, gconv, north, south, w_got, k_got, emb_got,
    emb, out, w_grad, k_grad,
    pad, taps,
):
    load_taps(ker, taps)

    def from_tiles(i):
        return [gconv[g, i] for g in range(CG)]

    def from_edge(ref):
        return lambda i: [ref[g, i].astype(F32) for g in range(CG)]

    @pl.loop(0, CAP)
    def _(t):
        spread(adj, t, pad, from_tiles, from_edge(north), from_edge(south))

    @pl.loop(0, CAP)
    def _(t):
        live = live_of(cnt, t)
        for g in range(CG):
            lanes = slice(g * 128, g * 128 + 128)
            rows = conv_tile(pad, taps, g, t, True)
            extra = pw[0, t] * cot[:, lanes] / TILE
            for a in range(TILE):
                g_out = live * (up[t, a, :, lanes].astype(F32) + extra)
                out[t, a, :, lanes] = (live * (g_out + rows[a])).astype(BF16)

    emb[...] = emb_got[0:1]
    for k in range(8):
        w_grad[k * 3 : k * 3 + 3, :] = w_got[k].astype(F32)
    for ij in range(49):
        k_grad[ij // 7, ij % 7 : ij % 7 + 1, :] = k_got[ij // 4, ij % 4 : ij % 4 + 1, :].astype(F32)


VMEM = pl.BlockSpec(memory_space=pltpu.VMEM)
SMEM = pl.BlockSpec(memory_space=pltpu.SMEM)
HBM = pl.BlockSpec(memory_space=pl.ANY)


def vmem(shape, dtype):
    return pltpu.VMEM(shape, dtype)


def passed_along(value, axis, steps):
    count = lax.axis_size(axis)
    leading, last = (max(0, -steps), min(count, count - steps))
    return lax.ppermute(value, axis, [(source, source + steps) for source in range(leading, last)])


def per_device(
    tiles_in, upstream, pool_weight, slide_cot, adjacency, counts, kernel, norm_gain, w_in, w_out,
    layer_scale,
):
    own, up = tiles_in[0], upstream[0]
    adj = adjacency[0]
    north = passed_along(own[:, TILE - 3 :], "space", 1)
    south = passed_along(own[:, :3], "space", -1)
    spaces = lax.axis_size("space")
    struct = jax.ShapeDtypeStruct
    pad = vmem((CG, CAP, 14, 24, 128), F32)
    taps = vmem((CG, 49, 8, 128), F32)
    edge = (CG, CAP, 3, TILE, 128)

    grads, emb, gconv, first, last = pl.pallas_call(
        forward_backward,
        out_shape=(
            struct((2, 16, ROWS, C), BF16),
            struct((8, C), F32),
            struct((CG, CAP, TILE, TILE, 128), F32),
            struct(edge, BF16),
            struct(edge, BF16),
        ),
        in_specs=[SMEM] * 3 + [VMEM] * 8 + [HBM] * 2,
        out_specs=(VMEM,) * 5,
        scratch_shapes=[
            pad,
            taps,
            vmem((CG, CAP, TILE, TILE, 128), F32),
            vmem((CAP, 64, 128), F32),
            vmem((PIX, C), BF16),
            vmem((PIX, C), BF16),
            vmem((PIX, C), F32),
            vmem((C, HID), BF16),
            vmem((HID, C), BF16),
            pltpu.SemaphoreType.DMA((2,)),
        ],
        compiler_params=pltpu.CompilerParams(vmem_limit_bytes=40 << 20),
        name="forward_backward",
    )(
        pool_weight, adj, counts, own, north, south, up, slide_cot, kernel, norm_gain[None],
        layer_scale[None], w_in, w_out,
    )

    dma = pltpu.SemaphoreType.DMA
    north_g, south_g, w_got, k_got, emb_got = pl.pallas_call(
        functools.partial(reduce_kernel, spaces),
        out_shape=(
            struct(edge, BF16),
            struct(edge, BF16),
            struct((8, 3, C), BF16),
            struct((16, 4, C), BF16),
            struct((8, C), F32),
        ),
        in_specs=[VMEM] * 4,
        out_specs=(VMEM,) * 5,
        scratch_shapes=[
            vmem((16, ROWS, C), BF16),
            vmem((8, C), F32),
            vmem((16, ROWS, C), BF16),
            vmem((16, ROWS, C), BF16),
            vmem((8, C), F32),
            vmem((8, C), F32),
            vmem((16, 8, C), BF16),
            vmem((16, 8, C), BF16),
            vmem((3, C), BF16),
            vmem((4, C), BF16),
            vmem((8, C), F32),
            vmem((8, C), F32),
            dma((2,)), dma((2,)),
            dma((2,)), dma((2,)),
            dma((16,)), dma((16,)),
            dma((1,)), dma((1,)),
            dma((16,)), dma((16,)),
            dma((8,)), dma((8,)),
            dma((16,)), dma((16,)),
            dma((1,)), dma((1,)),
        ],
        compiler_params=pltpu.CompilerParams(
            collective_id=0, has_side_effects=True, vmem_limit_bytes=40 << 20
        ),
        name="reduce_gradients",
    )(first, last, grads, emb)

    embedding, grad_tiles, w_grad, k_grad = pl.pallas_call(
        back_kernel,
        out_shape=(
            struct((1, C), F32),
            struct((CAP, TILE, TILE, C), BF16),
            struct((24, C), F32),
            struct((7, 7, C), F32),
        ),
        in_specs=[SMEM] * 3 + [VMEM] * 9,
        out_specs=(VMEM,) * 4,
        scratch_shapes=[pad, taps],
        compiler_params=pltpu.CompilerParams(vmem_limit_bytes=40 << 20),
        name="back",
    )(
        pool_weight, adj, counts, up, slide_cot, kernel, gconv, north_g, south_g, w_got, k_got,
        emb_got,
    )
    return embedding, grad_tiles[None], w_grad, k_grad


def solution(mesh):
    return jax.shard_map(
        per_device,
        mesh=mesh,
        in_specs=(
            P("dp", "space", None, None, None),
            P("dp", "space", None, None, None),
            P("dp", "space"),
            P("dp", None),
            P("dp", "space", None),
            P("dp", "space"),
            P(),
            P(),
            P(),
            P(),
            P(),
        ),
        out_specs=(P("dp", None), P("dp", "space", None, None, None), P("space", None), P()),
        check_vma=False,
    )
```

time: 447 us -> 78.5 us (0.18)
  the two profiles are of different devices: /device:TPU:24 before, /device:TPU:60 now
where the time goes in v1:
time: 78.5 us; the launch traced here: 78.1 us
  Pallas kernels  61.6 us (78%)
  local copies, waits for them, and re-layouts  9.61 us (12%)
  starting transfers between devices  4.33 us (6%)
  between operations  1.34 us (2%)
  waiting for transfers between devices  1.24 us (2%)
    pallas_call x1, Pallas kernels, per_device(): pl.pallas_call(functools.partial(reduce_kernel, spaces), out_shape=(struc...  50.2 us
    pallas_call x1, Pallas kernels, per_device(): pl.pallas_call(forward_backward, out_shape=(struct((2, 16, ROWS, C), BF16...  8.11 us
    unnamed x18, local copies, waits for them, and re-layouts  7.3 us
    ppermute x2, starting transfers between devices, passed_along(): lax.ppermute(value, axis, [(source, source + steps) for source in range(l...  4.33 us
    pallas_call x1, Pallas kernels, per_device(): pl.pallas_call(back_kernel, out_shape=(struct((1, C), F32), struct((CAP,...  3.28 us
  transfers between devices with their start and end apart: 2, of which 1 were waited for; matrix products, arithmetic and copies ran while one was open for 2% of the time, Pallas kernels for 0%

profile of v1, /device:TPU:60, one launch (start us, length us, event | category | flops | bytes accessed | tf_op | source)
XLA Modules:
  0.0 78.1 jit_solution(15314880114393596139)
XLA Ops:
  0.6 0.9 %fusion = (bf16[4,3,8,384]{3,2,1,0:T(8,128)(2,1)S(1)}, bf16[4,3,8,384]{3,2,1,0:T(8,128)(2,1)S(1)}) fusion(bf16[4,8,8,384]{3,2,1,0:T(8,128)(2,1)} %bitcast.6), kind=kLoop, calls=%fused_computation | loop fusion | bytes 294912 | tf_op jit(solution)/shard_map/slice | solution.py:438
  1.6 1.9 %collective-permute-start.1 = (bf16[4,3,8,384]{3,2,1,0:T(8,128)(2,1)S(1)}, bf16[4,3,8,384]{3,2,1,0:T(8,128)(2,1)S(1)}, u32[]{:S(2)}, u32[]{:S(2)}) collective-permute-start(bf16[4,3,8,384]{3,2,1,0:T(8,128)(2,1)S(1)} %get-tuple-element.32), channel_id=1, source_target_pairs={{1,0},{2,1},{3,2},{4,3},{5,4},{6,5},{7,6},{8,7},{9,8},{10,9},{11,1... | collective-permute-start | bytes 221192 | tf_op jit(solution)/shard_map/ppermute | solution.py:428
  3.5 2.4 %collective-permute-start = (bf16[4,3,8,384]{3,2,1,0:T(8,128)(2,1)S(1)}, bf16[4,3,8,384]{3,2,1,0:T(8,128)(2,1)S(1)}, u32[]{:S(2)}, u32[]{:S(2)}) collective-permute-start(bf16[4,3,8,384]{3,2,1,0:T(8,128)(2,1)S(1)} %get-tuple-element.33), channel_id=1, source_target_pairs={{0,1},{1,2},{2,3},{3,4},{4,5},{5,6},{6,7},{7,8},{8,9},{9,10},{10,1... | collective-permute-start | bytes 221192 | tf_op jit(solution)/shard_map/ppermute | solution.py:428
  6.6 0.7 broadcast_in_dim.9.gain
  7.3 0.7 broadcast_in_dim.10.scale
  7.9 0.0 collective-permute-done.1.south
  7.9 1.2 %collective-permute-done.north = bf16[4,3,8,384]{3,2,1,0:T(8,128)(2,1)S(1)} collective-permute-done((bf16[4,3,8,384]{3,2,1,0:T(8,128)(2,1)S(1)}, bf16[4,3,8,384]{3,2,1,0:T(8,128)(2,1)S(1)}, u32[]{:S(2)}, u32[]{:S(2)}) %collective-permute-start) | collective-permute-done | bytes 73760 | tf_op jit(solution)/shard_map/ppermute | solution.py:428
  9.2 0.0 copy-start
  9.2 1.3 %copy-done = bf16[384,1536]{1,0:T(8,128)(2,1)S(1)} copy-done((bf16[384,1536]{1,0:T(8,128)(2,1)S(1)}, bf16[384,1536]{1,0:T(8,128)(2,1)}, u32[]{:S(2)}) %copy-start) | copy-done | bytes 1179672
  10.4 0.0 copy-start.1
  10.5 1.3 %copy-done.1 = bf16[1536,384]{1,0:T(8,128)(2,1)S(1)} copy-done((bf16[1536,384]{1,0:T(8,128)(2,1)S(1)}, bf16[1536,384]{1,0:T(8,128)(2,1)}, u32[]{:S(2)}) %copy-start.1) | copy-done | bytes 1179672
  11.7 0.0 copy-start.2
  11.7 0.9 %copy-done.2 = bf16[1,4,8,8,384]{4,3,2,1,0:T(8,128)(2,1)S(1)} copy-done((bf16[1,4,8,8,384]{4,3,2,1,0:T(8,128)(2,1)S(1)}, bf16[1,4,8,8,384]{4,3,2,1,0:T(8,128)(2,1)}, u32[]{:S(2)}) %copy-start.2) | copy-done | bytes 196632
  12.6 0.0 copy-start.4
  12.6 0.9 %copy-done.4 = bf16[1,4,8,8,384]{4,3,2,1,0:T(8,128)(2,1)S(1)} copy-done((bf16[1,4,8,8,384]{4,3,2,1,0:T(8,128)(2,1)S(1)}, bf16[1,4,8,8,384]{4,3,2,1,0:T(8,128)(2,1)}, u32[]{:S(2)}) %copy-start.4) | copy-done | bytes 196632
  13.6 0.0 copy-start.5
  13.6 0.9 %copy-done.5 = f32[7,7,384]{2,1,0:T(8,128)S(1)} copy-done((f32[7,7,384]{2,1,0:T(8,128)S(1)}, f32[7,7,384]{2,1,0:T(8,128)}, u32[]{:S(2)}) %copy-start.5) | copy-done | bytes 75288
  14.5 0.0 copy-start.6
  14.5 0.7 copy-done.6
  15.1 0.0 copy-start.7
  15.1 0.7 copy-done.7
  15.8 0.0 copy-start.8
  15.8 0.7 copy-done.8
  16.5 8.1 %forward_backward.1 = (bf16[2,16,52,384]{3,2,1,0:T(8,128)(2,1)S(1)}, f32[8,384]{1,0:T(8,128)S(1)}, f32[3,4,8,8,128]{4,3,2,1,0:T(8,128)S(1)}, bf16[3,4,3,8,128]{4...) custom-call(f32[1,4]{1,0:T(1,128)S(1)} %copy-done.8, s32[4,8]{1,0:T(4,128)S(1)} %bitcast.8, s32[1,1]{1,0:T(1,128)S(6)} %copy.15.cnt, ...), custom_call_target="tpu_custom_call" | custom-call | tf_op jit(solution)/shard_map/forward_backward/pallas_call | solution.py:445
  24.6 0.0 copy-start.3
  24.6 50.2 %reduce_gradients.1 = (bf16[3,4,3,8,128]{4,3,2,1,0:T(8,128)(2,1)S(1)}, bf16[3,4,3,8,128]{4,3,2,1,0:T(8,128)(2,1)S(1)}, bf16[8,3,384]{2,1,0:T(4,128)(2,1)S(1)}, b...) custom-call(bf16[3,4,3,8,128]{4,3,2,1,0:T(8,128)(2,1)S(1)} %get-tuple-element.19.first, ...), custom_call_target="tpu_custom_call" | custom-call | tf_op jit(solution)/shard_map/reduce_gradients/pallas_call | solution.py:476
  74.8 0.0 copy-done.3
  74.8 3.3 %back.1 = (f32[1,384]{1,0:T(1,128)}, bf16[4,8,8,384]{3,2,1,0:T(8,128)(2,1)}, f32[24,384]{1,0:T(8,128)}, f32[7,7,384]{2,1,0:T(8,128)}) custom-call(f32[1,4]{1,0:T(1,128)S(1)} %copy-done.8, s32[4,8]{1,0:T(4,128)S(1)} %bitcast.9, s32[1,1]{1,0:T(1,128)S(6)} %copy.15.cnt, bf16[4,8,8,384]{3,2,1,0:T(8,128)(2,1)S(1)} %bitcast.5, f32[1,384]{1,0:T(1,128)S(1)} %copy-done.7, ...), custom_call_target="tpu_custom_call" | custom-call | tf_op jit(solution)/shard_map/back/pallas_call | solution.py:515
Async XLA Ops:
  1.6 6.4 %collective-permute-start.1 = (bf16[4,3,8,384]{3,2,1,0:T(8,128)(2,1)S(1)}, bf16[4,3,8,384]{3,2,1,0:T(8,128)(2,1)S(1)}, u32[]{:S(2)}, u32[]{:S(2)}) collective-permute-start(bf16[4,3,8,384]{3,2,1,0:T(8,128)(2,1)S(1)} %get-tuple-element.32), channel_id=1, source_target_pairs={{1,0},{2,1},{3,2},{4,3},{5,4},{6,5},{7,6},{8,7},{9,8},{10,9},{11,1... | collective-permute-start | bytes 221192 | tf_op jit(solution)/shard_map/ppermute | solution.py:428
  3.5 5.7 %collective-permute-start = (bf16[4,3,8,384]{3,2,1,0:T(8,128)(2,1)S(1)}, bf16[4,3,8,384]{3,2,1,0:T(8,128)(2,1)S(1)}, u32[]{:S(2)}, u32[]{:S(2)}) collective-permute-start(bf16[4,3,8,384]{3,2,1,0:T(8,128)(2,1)S(1)} %get-tuple-element.33), channel_id=1, source_target_pairs={{0,1},{1,2},{2,3},{3,4},{4,5},{5,6},{6,7},{7,8},{8,9},{9,10},{10,1... | collective-permute-start | bytes 221192 | tf_op jit(solution)/shard_map/ppermute | solution.py:428
  9.2 1.3 %copy-start = (bf16[384,1536]{1,0:T(8,128)(2,1)S(1)}, bf16[384,1536]{1,0:T(8,128)(2,1)}, u32[]{:S(2)}) copy-start(bf16[384,1536]{1,0:T(8,128)(2,1)} %w_in_hbm.1) | copy-start | bytes 3538948
  10.4 1.3 %copy-start.1 = (bf16[1536,384]{1,0:T(8,128)(2,1)S(1)}, bf16[1536,384]{1,0:T(8,128)(2,1)}, u32[]{:S(2)}) copy-start(bf16[1536,384]{1,0:T(8,128)(2,1)} %w_out_hbm.1) | copy-start | bytes 3538948
  11.7 0.9 %copy-start.2 = (bf16[1,4,8,8,384]{4,3,2,1,0:T(8,128)(2,1)S(1)}, bf16[1,4,8,8,384]{4,3,2,1,0:T(8,128)(2,1)}, u32[]{:S(2)}) copy-start(bf16[1,4,8,8,384]{4,3,2,1,0:T(8,128)(2,1)} %param.12) | copy-start | bytes 589828
  12.6 0.9 %copy-start.4 = (bf16[1,4,8,8,384]{4,3,2,1,0:T(8,128)(2,1)S(1)}, bf16[1,4,8,8,384]{4,3,2,1,0:T(8,128)(2,1)}, u32[]{:S(2)}) copy-start(bf16[1,4,8,8,384]{4,3,2,1,0:T(8,128)(2,1)} %param.11) | copy-start | bytes 589828
  13.6 0.9 %copy-start.5 = (f32[7,7,384]{2,1,0:T(8,128)S(1)}, f32[7,7,384]{2,1,0:T(8,128)}, u32[]{:S(2)}) copy-start(f32[7,7,384]{2,1,0:T(8,128)} %ker.3) | copy-start | bytes 225796
  14.5 0.7 copy-start.6
  15.1 0.7 copy-start.7
  15.8 0.7 copy-start.8
  24.6 50.2 %copy-start.3 = (bf16[1,4,8,8,384]{4,3,2,1,0:T(8,128)(2,1)S(1)}, bf16[1,4,8,8,384]{4,3,2,1,0:T(8,128)(2,1)}, u32[]{:S(2)}) copy-start(bf16[1,4,8,8,384]{4,3,2,1,0:T(8,128)(2,1)} %param.12) | copy-start | bytes 589828

commit v2 on v1

v2 whole, which is shorter than its diff:
```python
import functools

import jax
import jax.numpy as jnp
from jax import lax
from jax.experimental import pallas as pl
from jax.experimental.pallas import tpu as pltpu
from jax.sharding import PartitionSpec as P

MESH = pl.DeviceIdType.MESH
F32, BF16 = jnp.float32, jnp.bfloat16
sqrt_half = 0.7071067811865476
inv_root_two_pi = 0.3989422804014327

C, HID, CAP, TILE = 384, 1536, 4, 8
CG = C // 128
PIX = CAP * TILE * TILE
CHUNK = 384


def spread(adj, t, pad, own, north, south):
    def entry(e):
        wanted = adj[t, e]
        return jnp.bitwise_and(jnp.maximum(wanted, 0), CAP - 1), wanted >= 0

    parts = (
        (3, 8, (own, 2), (own, None), (own, 3)),
        (0, 3, (north, 4), (north, 0), (north, 5)),
        (11, 3, (south, 6), (south, 1), (south, 7)),
    )
    for row, rows, *columns in parts:
        for place, (source, e) in enumerate(columns):
            if e is None:
                groups = source(t)
            else:
                index, valid = entry(e)
                groups = [jnp.where(valid, g, 0.0) for g in source(index)]
            for g in range(CG):
                pad[g, t, row : row + rows, 8 * place : 8 * place + 8, :] = groups[g]


def conv_tile(pad, taps, g, t, flip):
    total = [None] * TILE
    for j in range(7):
        column = [taps[g, 48 - (i * 7 + j) if flip else i * 7 + j] for i in range(7)]
        for r in range(14):
            window = pad[g, t, r, 5 + j : 13 + j, :]
            for i in range(7):
                a = r - i
                if 0 <= a < TILE:
                    term = window * column[i]
                    total[a] = term if total[a] is None else total[a] + term
    return total


def split_groups(value):
    return [value[..., g * 128 : (g + 1) * 128] for g in range(CG)]


def live_of(cnt, t):
    return jnp.where(t < cnt[0, 0], 1.0, 0.0).astype(F32)


def grad_out_of(up, pw, cot, live, t):
    extra = pw[0, t] * cot[...] / TILE
    return live * (up[t].astype(F32) + extra[None])


def load_taps(ker, taps):
    for ij in range(49):
        row = ker[ij // 7, ij % 7 : ij % 7 + 1, :]
        for g in range(CG):
            taps[g, ij] = jnp.broadcast_to(row[:, g * 128 : (g + 1) * 128], (8, 128))


def copy_to(device, src, dst, send, recv):
    return pltpu.make_async_remote_copy(
        src_ref=src, dst_ref=dst, send_sem=send, recv_sem=recv,
        device_id=device, device_id_type=MESH,
    )


def greet(device):
    pl.semaphore_signal(
        pltpu.get_barrier_semaphore(), inc=1, device_id=device, device_id_type=MESH
    )


def halo_kernel(spaces, own, north, south, send, recv):
    dp, space = lax.axis_index("dp"), lax.axis_index("space")
    before = (dp, lax.rem(space + spaces - 1, spaces))
    after = (dp, lax.rem(space + 1, spaces))
    greet(before)
    greet(after)
    pl.semaphore_wait(pltpu.get_barrier_semaphore(), 2)
    down = copy_to(after, own.at[:, TILE - 3 :], north, send.at[0], recv.at[0])
    up = copy_to(before, own.at[:, :3], south, send.at[1], recv.at[1])
    down.start()
    up.start()
    down.wait()
    up.wait()


def main_kernel(
    spaces,
    pw, adj, cnt,
    own_in, north_in, south_in, up_in, cot_in, ker_in, gain_in, scale_in, w_in_in, w_out_in,
    out, got4, emb_out,
    own, north, south, up, cot, ker, gain, scale, w_in, w_out, load_sems,
    pad, pad_g, taps, normed, inv, lifted, gmix, glift, slope, gconv, kparts,
    grads, got1, send2, got2, kgrads, kgot1, ksend2, kgot2,
    emb, emb1, emb_sum, emb2, send3, got3, send4, half, other,
    edge_first, edge_last, north_g, south_g,
    s_halo, r_halo, s1, r1, s1k, r1k, s2, r2, s2k, r2k, s_e, r_e, s3, r3, s4, r4, s5, r5,
):
    dp, space = lax.axis_index("dp"), lax.axis_index("space")
    core = lax.rem(space, 2)
    z = lax.rem(space // 2, 16)
    plane = space // 32
    spot = dp * 2 + plane

    def at(d, p, zz):
        return (d, (p * 16 + zz) * 2 + core)

    def chunk_device(q):
        return at(q // 2, lax.rem(q, 2), z)

    partner = (dp, space + 1 - 2 * core)
    before = (dp, lax.rem(space + spaces - 1, spaces))
    after = (dp, lax.rem(space + 1, spaces))

    loads = {}
    sources = (
        (own_in, own), (north_in, north), (south_in, south), (ker_in, ker), (gain_in, gain),
        (up_in, up), (cot_in, cot), (scale_in, scale), (w_in_in, w_in), (w_out_in, w_out),
    )
    for n, (src, dst) in enumerate(sources):
        loads[n] = pltpu.make_async_copy(src, dst, load_sems.at[n])
        loads[n].start()

    greet(partner)
    greet(before)
    greet(after)

    @pl.loop(1, 16)
    def _(k):
        greet(at(dp, plane, lax.rem(z + k, 16)))
        greet(chunk_device(lax.rem(spot + k, 16)))

    loads[3].wait()
    load_taps(ker, taps)
    for n in (0, 1, 2):
        loads[n].wait()

    def groups_of(ref):
        return lambda i: split_groups(ref[i].astype(F32))

    @pl.loop(0, CAP)
    def _(t):
        spread(adj, t, pad, groups_of(own), groups_of(north), groups_of(south))

    @pl.loop(0, CAP)
    def _(t):
        @pl.loop(0, CG)
        def _(g):
            rows = conv_tile(pad, taps, g, t, False)
            for a in range(TILE):
                normed[g, t, a] = rows[a]

    for n in (4, 5, 6, 7):
        loads[n].wait()
    emb_own = jnp.zeros((1, C), F32)
    for t in range(CAP):
        live = live_of(cnt, t)
        x = [normed[g, t].reshape(64, 128) for g in range(CG)]
        mean = jnp.sum(x[0] + x[1] + x[2], axis=-1, keepdims=True) / C
        x = [v - mean for v in x]
        var = jnp.sum(x[0] * x[0] + x[1] * x[1] + x[2] * x[2], axis=-1, keepdims=True) / C
        istd = jnp.broadcast_to(lax.rsqrt(var + 1e-06), (64, 128))
        inv[t] = istd
        here = slice(t * 64, t * 64 + 64)
        for g in range(CG):
            lanes = slice(g * 128, g * 128 + 128)
            n = x[g] * istd
            normed[g, t] = n.reshape(TILE, TILE, 128)
            lifted[here, lanes] = (n * gain[:, lanes]).astype(BF16)
        g_out = grad_out_of(up, pw, cot, live, t)
        gmix[here, :] = (g_out * scale[...][None]).astype(BF16).reshape(64, C)
        weight = live * pw[0, t]
        emb_own = emb_own + weight * jnp.sum(own[t].astype(F32).reshape(64, C), axis=0, keepdims=True)

    d = lax.broadcasted_iota(jnp.int32, (8, CHUNK), 1)
    d_core = jnp.where(d >= 192, 1, 0)
    d = d - 192 * d_core
    d_dp = jnp.zeros_like(d)
    for m in range(1, 8):
        d_dp = d_dp + jnp.where(d >= 24 * m, 1, 0)
    d = d - 24 * d_dp
    d_z = jnp.zeros_like(d)
    for m in range(1, 8):
        d_z = d_z + jnp.where(d >= 3 * m, 1, 0)
    d = d - 3 * d_z
    source = d_z * 48 + d_core * 24 + d_dp * 3 + d
    rows = lax.broadcasted_iota(jnp.int32, (CHUNK, CHUNK), 0)
    order = jnp.where(rows == source[0:1], 1.0, 0.0).astype(BF16)

    loads[8].wait()
    loads[9].wait()

    def pair_of(h):
        return copy_to(partner, grads.at[1 - core, h], got1.at[h], s1.at[h], r1.at[h])

    def plane_of(h, k):
        to = lax.rem(dp + k, 8)
        return copy_to(
            at(to, h // 2, z), send2.at[h, to], got2.at[spot, h % 2], s2.at[h, k],
            r2.at[spot, h % 2],
        )

    def pass_on(h):
        pair_of(h).wait_recv()
        send2[h] = (grads[core, h].astype(F32) + got1[h].astype(F32)).astype(BF16)

        @pl.loop(1, 8)
        def _(k):
            plane_of(h, k).start()

        @pl.when(plane == h // 2)
        def _():
            got2[spot, h % 2] = send2[h, dp]

        @pl.when(plane != h // 2)
        def _():
            plane_of(h, 0).start()

    mixed = jnp.zeros((8, C), F32)
    for h in range(HID // CHUNK):
        here = slice(h * CHUNK, (h + 1) * CHUNK)
        pre = jnp.dot(lifted[...], w_in[:, here], preferred_element_type=F32)
        cdf = 0.5 * (1.0 + lax.erf(pre * sqrt_half))
        act = (pre * cdf).astype(BF16)
        density = jnp.exp(-0.5 * pre * pre) * inv_root_two_pi
        slope[:, here] = cdf + pre * density
        sent = jnp.dot(act, order, preferred_element_type=F32).astype(BF16)
        gw = lax.dot_general(
            sent, gmix[...], (((0,), (0,)), ((), ())), preferred_element_type=F32
        ).astype(BF16)
        for c in range(2):
            for m in range(8):
                grads[c, h, m] = gw[(c * 8 + m) * 24 : (c * 8 + m) * 24 + 24]
        if h == 0:
            pl.semaphore_wait(pltpu.get_barrier_semaphore(), 33)
        pair_of(h).start()
        pooled = jnp.zeros((1, CHUNK), F32)
        for t in range(CAP):
            weight = live_of(cnt, t) * pw[0, t]
            pooled = pooled + weight * jnp.sum(
                act[t * 64 : t * 64 + 64].astype(F32), axis=0, keepdims=True
            )
        high = pooled.astype(BF16)
        rest = pooled - high.astype(F32)
        middle = rest.astype(BF16)
        low = (rest - middle.astype(F32)).astype(BF16)
        three = jnp.concatenate([high, middle, low, jnp.zeros((5, CHUNK), BF16)], axis=0)
        mixed = mixed + jnp.dot(three, w_out[here, :], preferred_element_type=F32)
        if h > 0:
            pass_on(h - 1)
    mix = jnp.sum(mixed, axis=0, keepdims=True)
    emb[...] = jnp.broadcast_to((emb_own + scale[...] * mix) / TILE, (8, C))
    emb_pair = copy_to(partner, emb, emb1, s_e.at[0], r_e.at[0])
    emb_pair.start()

    for h in range(HID // CHUNK):
        here = slice(h * CHUNK, (h + 1) * CHUNK)
        gact = lax.dot_general(
            gmix[...], w_out[here, :], (((1,), (1,)), ((), ())), preferred_element_type=F32
        )
        gpre = (gact * slope[:, here]).astype(BF16)
        gl = lax.dot_general(
            gpre, w_in[:, here], (((1,), (1,)), ((), ())), preferred_element_type=F32
        )
        if h == 0:
            glift[...] = gl
            pass_on(HID // CHUNK - 1)
        else:
            glift[...] += gl

    for t in range(CAP):
        here = slice(t * 64, t * 64 + 64)
        gn = [glift[here, g * 128 : g * 128 + 128] * gain[:, g * 128 : g * 128 + 128] for g in range(CG)]
        n = [normed[g, t].reshape(64, 128) for g in range(CG)]
        m1 = jnp.sum(gn[0] + gn[1] + gn[2], axis=-1, keepdims=True) / C
        m2 = jnp.sum(gn[0] * n[0] + gn[1] * n[1] + gn[2] * n[2], axis=-1, keepdims=True) / C
        for g in range(CG):
            gc = (inv[t] * (gn[g] - m1 - n[g] * m2)).reshape(TILE, TILE, 128)
            gconv[g, t] = gc
            edge_first[g, t] = gc[:3].astype(BF16)
            edge_last[g, t] = gc[TILE - 3 :].astype(BF16)
    to_after = copy_to(after, edge_last, north_g, s_halo.at[0], r_halo.at[0])
    to_before = copy_to(before, edge_first, south_g, s_halo.at[1], r_halo.at[1])
    to_after.start()
    to_before.start()

    emb_pair.wait_recv()
    emb_sum[...] = emb[...] + emb1[...]
    across = copy_to(at(dp, 1 - plane, z), emb_sum, emb2, s_e.at[1], r_e.at[1])
    across.start()

    @pl.loop(0, CG)
    def _(g):
        for j in range(7):

            def tile_taps(t, carry, j=j):
                gc = [gconv[g, t, a] for a in range(TILE)]
                total = list(carry)
                for r in range(14):
                    window = pad[g, t, r, 5 + j : 13 + j, :]
                    for i in range(7):
                        a = r - i
                        if 0 <= a < TILE:
                            total[i] = total[i] + window * gc[a]
                return tuple(total)

            sums = lax.fori_loop(
                0, CAP, tile_taps, tuple(jnp.zeros((8, 128), F32) for _ in range(7))
            )
            for i in range(7):
                kparts[g, i * 7 + j] = sums[i]

    for g in range(CG):
        lanes = slice(g * 128, g * 128 + 128)
        total = jnp.sum(kparts[g], axis=1)
        total = jnp.concatenate([total, jnp.zeros((15, 128), F32)], axis=0)
        for q in range(16):
            kgrads[q, :, lanes] = total[q * 4 : q * 4 + 4].astype(BF16)
    kpair = copy_to(partner, kgrads, kgot1, s1k.at[0], r1k.at[0])
    kpair.start()

    def from_tiles(i):
        return [gconv[g, i] for g in range(CG)]

    def from_edge(ref):
        return lambda i: [ref[g, i].astype(F32) for g in range(CG)]

    def back(t):
        spread(adj, t, pad_g, from_tiles, from_edge(north_g), from_edge(south_g))
        live = live_of(cnt, t)
        for g in range(CG):
            lanes = slice(g * 128, g * 128 + 128)
            rows = conv_tile(pad_g, taps, g, t, True)
            extra = pw[0, t] * cot[:, lanes] / TILE
            for a in range(TILE):
                g_out = live * (up[t, a, :, lanes].astype(F32) + extra)
                out[t, a, :, lanes] = (live * (g_out + rows[a])).astype(BF16)

    to_after.wait_recv()
    to_before.wait_recv()

    def kplane(q, slot, k):
        return copy_to(chunk_device(q), ksend2.at[q], kgot2.at[slot], s2k.at[k], r2k.at[slot])

    @pl.loop(0, CAP)
    def _(t):
        back(t)

        @pl.when(t == 0)
        def _():
            kpair.wait_recv()
            ksend2[...] = (kgrads[...].astype(F32) + kgot1[...].astype(F32)).astype(BF16)

            @pl.loop(1, 16)
            def _(k):
                kplane(lax.rem(spot + k, 16), spot, k).start()

            kgot2[spot] = ksend2[spot]

    across.wait_recv()
    emb_both = emb_sum[0:1] + emb2[0:1]
    high = emb_both.astype(BF16).astype(F32)
    mine = jnp.where(core == 0, high, emb_both - high)
    for h in range(HID // CHUNK):
        pair_of(h).wait_send()
    emb_pair.wait_send()
    kpair.wait_send()
    to_after.wait_send()
    to_before.wait_send()

    @pl.loop(1, 16)
    def _(k):
        q = lax.rem(spot + k, 16)
        kplane(q, q, k).wait_recv()
        for hh in range(2):
            copy_to(partner, send2.at[0, 0], got2.at[q, hh], s2.at[0, 0], r2.at[q, hh]).wait_recv()

    total = [got2[0, hh].astype(F32) for hh in range(2)]
    tail = kgot2[0].astype(F32)
    for q in range(1, 16):
        total = [total[hh] + got2[q, hh].astype(F32) for hh in range(2)]
        tail = tail + kgot2[q].astype(F32)

    for q in range(16):
        row = q % 8 * 3
        send3[q] = jnp.concatenate([total[q // 8][row : row + 3], tail, mine], axis=0).astype(BF16)

    def ring(q, slot, k):
        return copy_to(at(dp, plane, q), send3.at[q], got3.at[slot], s3.at[k], r3.at[slot])

    @pl.loop(1, 16)
    def _(k):
        ring(lax.rem(z + k, 16), z, k).start()

    got3[z] = send3[z]
    across.wait_send()
    for h in range(HID // CHUNK):

        @pl.loop(1, 8)
        def _(k):
            plane_of(h, k).wait_send()

        @pl.when(plane != h // 2)
        def _():
            plane_of(h, 0).wait_send()

    @pl.loop(1, 16)
    def _(k):
        q = lax.rem(spot + k, 16)
        kplane(q, q, k).wait_send()

    @pl.loop(1, 16)
    def _(k):
        q = lax.rem(z + k, 16)
        ring(q, q, k).wait_recv()

    total = got3[0].astype(F32)
    for q in range(1, 16):
        total = total + got3[q].astype(F32)

    send4[...] = total.astype(BF16)
    half[...] = jnp.broadcast_to(total[7:8], (8, C))

    def last(q, slot, k):
        return copy_to(chunk_device(q), send4, got4.at[slot], s4.at[k], r4.at[slot])

    @pl.loop(1, 16)
    def _(k):
        last(lax.rem(spot + k, 16), spot, k).start()

    swap = copy_to(partner, half, other, s5.at[0], r5.at[0])
    swap.start()
    got4[spot] = send4[...]

    @pl.loop(1, 16)
    def _(k):
        q = lax.rem(z + k, 16)
        ring(q, q, k).wait_send()

    swap.wait()
    emb_out[...] = half[...] + other[...]

    @pl.loop(1, 16)
    def _(k):
        q = lax.rem(spot + k, 16)
        last(q, q, k).wait()


def finish_kernel(out, got4, emb_got, emb, tiles, w_grad, k_grad):
    plane = lax.axis_index("space") // 32
    tiles[...] = out[...]
    emb[...] = emb_got[0:1]
    for d in range(8):
        w_grad[d * 3 : d * 3 + 3, :] = got4[d * 2 + plane, 0:3].astype(F32)
    for ij in range(49):
        row = got4[ij // 4, 3 + ij % 4 : 4 + ij % 4].astype(F32)
        k_grad[ij // 7, ij % 7 : ij % 7 + 1, :] = row


VMEM = pl.BlockSpec(memory_space=pltpu.VMEM)
SMEM = pl.BlockSpec(memory_space=pltpu.SMEM)
HBM = pl.BlockSpec(memory_space=pltpu.HBM)


def vmem(shape, dtype):
    return pltpu.VMEM(shape, dtype)


def per_device(
    tiles_in, upstream, pool_weight, slide_cot, adjacency, counts, kernel, norm_gain, w_in, w_out,
    layer_scale,
):
    own, up = tiles_in[0], upstream[0]
    spaces = lax.axis_size("space")
    struct = jax.ShapeDtypeStruct
    dma = pltpu.SemaphoreType.DMA
    edge = (CG, CAP, 3, TILE, 128)
    halo = (CAP, 3, TILE, C)
    blocks = (CG, CAP, TILE, TILE, 128)
    chunks = HID // CHUNK

    north, south = pl.pallas_call(
        functools.partial(halo_kernel, spaces),
        out_shape=(struct(halo, BF16), struct(halo, BF16)),
        in_specs=[HBM],
        out_specs=(HBM, HBM),
        scratch_shapes=[dma((2,)), dma((2,))],
        compiler_params=pltpu.CompilerParams(collective_id=0, has_side_effects=True),
        name="halo",
    )(own)

    out, got4, emb = pl.pallas_call(
        functools.partial(main_kernel, spaces),
        out_shape=(
            struct((CAP, TILE, TILE, C), BF16),
            struct((16, 8, C), BF16),
            struct((8, C), F32),
        ),
        in_specs=[SMEM] * 3 + [HBM] * 10,
        out_specs=(VMEM,) * 3,
        scratch_shapes=[
            vmem((CAP, TILE, TILE, C), BF16),
            vmem(halo, BF16),
            vmem(halo, BF16),
            vmem((CAP, TILE, TILE, C), BF16),
            vmem((1, C), F32),
            vmem((7, 7, C), F32),
            vmem((1, C), F32),
            vmem((1, C), F32),
            vmem((C, HID), BF16),
            vmem((HID, C), BF16),
            dma((10,)),
            vmem((CG, CAP, 14, 24, 128), F32),
            vmem((CG, CAP, 14, 24, 128), F32),
            vmem((CG, 49, 8, 128), F32),
            vmem(blocks, F32),
            vmem((CAP, 64, 128), F32),
            vmem((PIX, C), BF16),
            vmem((PIX, C), BF16),
            vmem((PIX, C), F32),
            vmem((PIX, HID), F32),
            vmem(blocks, F32),
            vmem((CG, 49, 8, 128), F32),
            vmem((2, chunks, 8, 24, C), BF16),
            vmem((chunks, 8, 24, C), BF16),
            vmem((chunks, 8, 24, C), BF16),
            vmem((16, 2, 24, C), BF16),
            vmem((16, 4, C), BF16),
            vmem((16, 4, C), BF16),
            vmem((16, 4, C), BF16),
            vmem((16, 4, C), BF16),
            vmem((8, C), F32),
            vmem((8, C), F32),
            vmem((8, C), F32),
            vmem((8, C), F32),
            vmem((16, 8, C), BF16),
            vmem((16, 8, C), BF16),
            vmem((8, C), BF16),
            vmem((8, C), F32),
            vmem((8, C), F32),
            vmem(edge, BF16),
            vmem(edge, BF16),
            vmem(edge, BF16),
            vmem(edge, BF16),
            dma((2,)), dma((2,)),
            dma((chunks,)), dma((chunks,)),
            dma((1,)), dma((1,)),
            dma((chunks, 8)), dma((16, 2)),
            dma((16,)), dma((16,)),
            dma((2,)), dma((2,)),
            dma((16,)), dma((16,)),
            dma((16,)), dma((16,)),
            dma((1,)), dma((1,)),
        ],
        compiler_params=pltpu.CompilerParams(
            collective_id=1, has_side_effects=True, vmem_limit_bytes=48 << 20
        ),
        name="main",
    )(
        pool_weight, adjacency[0], counts, own, north, south, up, slide_cot, kernel,
        norm_gain[None], layer_scale[None], w_in, w_out,
    )

    embedding, grad_tiles, w_grad, k_grad = pl.pallas_call(
        finish_kernel,
        out_shape=(
            struct((1, C), F32),
            struct((CAP, TILE, TILE, C), BF16),
            struct((24, C), F32),
            struct((7, 7, C), F32),
        ),
        in_specs=[VMEM] * 3,
        out_specs=(VMEM,) * 4,
        name="finish",
    )(out, got4, emb)
    return embedding, grad_tiles[None], w_grad, k_grad


def solution(mesh):
    return jax.shard_map(
        per_device,
        mesh=mesh,
        in_specs=(
            P("dp", "space", None, None, None),
            P("dp", "space", None, None, None),
            P("dp", "space"),
            P("dp", None),
            P("dp", "space", None),
            P("dp", "space"),
            P(),
            P(),
            P(),
            P(),
            P(),
        ),
        out_specs=(P("dp", None), P("dp", "space", None, None, None), P("space", None), P()),
        check_vma=False,
    )
```

time: 78.5 us -> 70.2 us (0.89)
  the two profiles are of different devices: /device:TPU:60 before, /device:TPU:24 now
where the time goes in v2:
time: 70.2 us; the launch traced here: 69.7 us
  Pallas kernels  56 us (80%)
  local copies, waits for them, and re-layouts  12.3 us (18%)
  between operations  1.32 us (2%)
    pallas_call x1, Pallas kernels, per_device(): pl.pallas_call(functools.partial(main_kernel, spaces), out_shape=(struct(...  41.4 us
    pallas_call x1, Pallas kernels, per_device(): pl.pallas_call(functools.partial(halo_kernel, spaces), out_shape=(struct(...  12.9 us
    unnamed x26, local copies, waits for them, and re-layouts  11 us
    pallas_call x1, Pallas kernels, per_device(): pl.pallas_call(finish_kernel, out_shape=(struct((1, C), F32), struct((CAP...  1.73 us

profile of v2, /device:TPU:24, one launch (start us, length us, event | category | flops | bytes accessed | tf_op | source)
XLA Modules:
  0.0 69.7 jit_solution(16375593487584183892)
XLA Ops:
  1.3 0.7 broadcast_in_dim.9.gain_in
  2.0 0.7 broadcast_in_dim.10.scale_in
  2.6 12.9 %halo.1 = (bf16[4,3,8,384]{3,2,1,0:T(8,128)(2,1)}, bf16[4,3,8,384]{3,2,1,0:T(8,128)(2,1)}) custom-call(bf16[4,8,8,384]{3,2,1,0:T(8,128)(2,1)} %bitcast.4), custom_call_target="tpu_custom_call" | custom-call | tf_op jit(solution)/shard_map/halo/pallas_call | solution.py:499
  15.5 0.0 copy-start
  15.5 1.3 %copy-done = bf16[384,1536]{1,0:T(8,128)(2,1)S(1)} copy-done((bf16[384,1536]{1,0:T(8,128)(2,1)S(1)}, bf16[384,1536]{1,0:T(8,128)(2,1)}, u32[]{:S(2)}) %copy-start) | copy-done | bytes 1179672
  16.8 0.0 copy-start.1
  16.8 1.3 %copy-done.1 = bf16[1536,384]{1,0:T(8,128)(2,1)S(1)} copy-done((bf16[1536,384]{1,0:T(8,128)(2,1)S(1)}, bf16[1536,384]{1,0:T(8,128)(2,1)}, u32[]{:S(2)}) %copy-start.1) | copy-done | bytes 1179672
  18.1 0.0 copy-start.2
  18.1 0.9 %copy-done.2 = bf16[1,4,8,8,384]{4,3,2,1,0:T(8,128)(2,1)S(1)} copy-done((bf16[1,4,8,8,384]{4,3,2,1,0:T(8,128)(2,1)S(1)}, bf16[1,4,8,8,384]{4,3,2,1,0:T(8,128)(2,1)}, u32[]{:S(2)}) %copy-start.2) | copy-done | bytes 196632
  19.0 0.0 copy-start.4
  19.0 0.9 %copy-done.4 = bf16[1,4,8,8,384]{4,3,2,1,0:T(8,128)(2,1)S(1)} copy-done((bf16[1,4,8,8,384]{4,3,2,1,0:T(8,128)(2,1)S(1)}, bf16[1,4,8,8,384]{4,3,2,1,0:T(8,128)(2,1)}, u32[]{:S(2)}) %copy-start.4) | copy-done | bytes 196632
  19.9 0.0 copy-start.6
  19.9 0.9 %copy-done.6 = f32[7,7,384]{2,1,0:T(8,128)S(1)} copy-done((f32[7,7,384]{2,1,0:T(8,128)S(1)}, f32[7,7,384]{2,1,0:T(8,128)}, u32[]{:S(2)}) %copy-start.6) | copy-done | bytes 75288
  20.8 0.0 copy-start.7
  20.8 0.9 %copy-done.7 = bf16[4,3,8,384]{3,2,1,0:T(8,128)(2,1)S(1)} copy-done((bf16[4,3,8,384]{3,2,1,0:T(8,128)(2,1)S(1)}, bf16[4,3,8,384]{3,2,1,0:T(8,128)(2,1)}, u32[]{:S(2)}) %copy-start.7) | copy-done | bytes 73752
  21.7 0.0 copy-start.8
  21.7 0.9 %copy-done.8 = bf16[4,3,8,384]{3,2,1,0:T(8,128)(2,1)S(1)} copy-done((bf16[4,3,8,384]{3,2,1,0:T(8,128)(2,1)S(1)}, bf16[4,3,8,384]{3,2,1,0:T(8,128)(2,1)}, u32[]{:S(2)}) %copy-start.8) | copy-done | bytes 73752
  22.6 0.0 copy-start.10
  22.6 0.7 copy-done.10
  23.3 0.0 copy-start.11
  23.3 0.7 copy-done.11
  24.0 0.0 copy-start.12
  24.0 0.7 copy-done.12
  24.6 41.4 %main.1 = (bf16[4,8,8,384]{3,2,1,0:T(8,128)(2,1)S(1)}, bf16[16,8,384]{2,1,0:T(8,128)(2,1)S(1)}, f32[8,384]{1,0:T(8,128)S(1)}) custom-call(f32[1,4]{1,0:T(1,128)S(1)} %copy-done.12, s32[4,8]{1,0:T(4,128)S(1)} %bitcast.7, s32[1,1]{1,0:T(1,128)S(6)} %copy.15.cnt, bf16[4,8,8,384]{3,2,1,0:T(8,128)(2,1)S(1)} %bitcast.5, bf16[4,3,8,384]{3,2,1,0:T(8,128)(2,1)S(1)} %copy-done.7, ...), custom_call_target="tpu_custom_call" | custom-call | tf_op jit(solution)/shard_map/main/pallas_call | solution.py:509
  66.0 0.0 copy-start.3
  66.0 0.7 copy-done.3
  66.7 0.0 copy-start.5
  66.7 0.6 copy-done.5
  67.3 0.0 copy-start.9
  67.3 0.6 copy-done.9
  67.9 1.7 %finish.1 = (f32[1,384]{1,0:T(1,128)}, bf16[4,8,8,384]{3,2,1,0:T(8,128)(2,1)}, f32[24,384]{1,0:T(8,128)}, f32[7,7,384]{2,1,0:T(8,128)}) custom-call(bf16[4,8,8,384]{3,2,1,0:T(8,128)(2,1)} %copy-done.3, bf16[16,8,384]{2,1,0:T(8,128)(2,1)} %copy-done.5, f32[8,384]{1,0:T(8,128)} %copy-done.9), custom_call_target="tpu_custom_call" | custom-call | tf_op jit(solution)/shard_map/finish/pallas_call | solution.py:581
Async XLA Ops:
  15.5 1.3 %copy-start = (bf16[384,1536]{1,0:T(8,128)(2,1)S(1)}, bf16[384,1536]{1,0:T(8,128)(2,1)}, u32[]{:S(2)}) copy-start(bf16[384,1536]{1,0:T(8,128)(2,1)} %w_in_in.1) | copy-start | bytes 3538948
  16.8 1.3 %copy-start.1 = (bf16[1536,384]{1,0:T(8,128)(2,1)S(1)}, bf16[1536,384]{1,0:T(8,128)(2,1)}, u32[]{:S(2)}) copy-start(bf16[1536,384]{1,0:T(8,128)(2,1)} %w_out_in.1) | copy-start | bytes 3538948
  18.1 0.9 %copy-start.2 = (bf16[1,4,8,8,384]{4,3,2,1,0:T(8,128)(2,1)S(1)}, bf16[1,4,8,8,384]{4,3,2,1,0:T(8,128)(2,1)}, u32[]{:S(2)}) copy-start(bf16[1,4,8,8,384]{4,3,2,1,0:T(8,128)(2,1)} %param.11) | copy-start | bytes 589828
  19.0 0.9 %copy-start.4 = (bf16[1,4,8,8,384]{4,3,2,1,0:T(8,128)(2,1)S(1)}, bf16[1,4,8,8,384]{4,3,2,1,0:T(8,128)(2,1)}, u32[]{:S(2)}) copy-start(bf16[1,4,8,8,384]{4,3,2,1,0:T(8,128)(2,1)} %param.12) | copy-start | bytes 589828
  19.9 0.9 %copy-start.6 = (f32[7,7,384]{2,1,0:T(8,128)S(1)}, f32[7,7,384]{2,1,0:T(8,128)}, u32[]{:S(2)}) copy-start(f32[7,7,384]{2,1,0:T(8,128)} %ker_in.1) | copy-start | bytes 225796
  20.8 0.9 %copy-start.7 = (bf16[4,3,8,384]{3,2,1,0:T(8,128)(2,1)S(1)}, bf16[4,3,8,384]{3,2,1,0:T(8,128)(2,1)}, u32[]{:S(2)}) copy-start(bf16[4,3,8,384]{3,2,1,0:T(8,128)(2,1)} %get-tuple-element.13.north_in) | copy-start | bytes 221188
  21.7 0.9 %copy-start.8 = (bf16[4,3,8,384]{3,2,1,0:T(8,128)(2,1)S(1)}, bf16[4,3,8,384]{3,2,1,0:T(8,128)(2,1)}, u32[]{:S(2)}) copy-start(bf16[4,3,8,384]{3,2,1,0:T(8,128)(2,1)} %get-tuple-element.14.south_in) | copy-start | bytes 221188
  22.6 0.7 copy-start.10
  23.3 0.7 copy-start.11
  24.0 0.7 copy-start.12
  66.0 0.7 copy-start.3
  66.7 0.6 copy-start.5
  67.3 0.6 copy-start.9

commit v3 on v2

--- a/solution.py
+++ b/solution.py
@@ -1,3 +1,4 @@
+import contextlib
 import functools
 
 import jax
@@ -16,6 +17,12 @@
 CG = C // 128
 PIX = CAP * TILE * TILE
 CHUNK = 384
+VMEM_BYTES = 60 << 20
+SCOPES = False
+
+
+def scope(name):
+    return jax.named_scope(name) if SCOPES else contextlib.nullcontext()
 
 
 def spread(adj, t, pad, own, north, south):
@@ -23,11 +30,12 @@
         wanted = adj[t, e]
         return jnp.bitwise_and(jnp.maximum(wanted, 0), CAP - 1), wanted >= 0
 
-    parts = (
-        (3, 8, (own, 2), (own, None), (own, 3)),
-        (0, 3, (north, 4), (north, 0), (north, 5)),
-        (11, 3, (south, 6), (south, 1), (south, 7)),
-    )
+    parts = []
+    if own is not None:
+        parts.append((3, 8, (own, 2), (own, None), (own, 3)))
+    if north is not None:
+        parts.append((0, 3, (north, 4), (north, 0), (north, 5)))
+        parts.append((11, 3, (south, 6), (south, 1), (south, 7)))
     for row, rows, *columns in parts:
         for place, (source, e) in enumerate(columns):
             if e is None:
@@ -86,32 +94,17 @@
     )
 
 
-def halo_kernel(spaces, own, north, south, send, recv):
-    dp, space = lax.axis_index("dp"), lax.axis_index("space")
-    before = (dp, lax.rem(space + spaces - 1, spaces))
-    after = (dp, lax.rem(space + 1, spaces))
-    greet(before)
-    greet(after)
-    pl.semaphore_wait(pltpu.get_barrier_semaphore(), 2)
-    down = copy_to(after, own.at[:, TILE - 3 :], north, send.at[0], recv.at[0])
-    up = copy_to(before, own.at[:, :3], south, send.at[1], recv.at[1])
-    down.start()
-    up.start()
-    down.wait()
-    up.wait()
-
-
 def main_kernel(
     spaces,
     pw, adj, cnt,
-    own_in, north_in, south_in, up_in, cot_in, ker_in, gain_in, scale_in, w_in_in, w_out_in,
-    out, got4, emb_out,
-    own, north, south, up, cot, ker, gain, scale, w_in, w_out, load_sems,
-    pad, pad_g, taps, normed, inv, lifted, gmix, glift, slope, gconv, kparts,
+    own_in, up_in, cot_in, ker_in, gain_in, scale_in, w_in_in, w_out_in,
+    out_hbm, got4, emb_hbm,
+    out, emb_out, out_sems, own, north, south, up, cot, ker, gain, scale, w_in, w_out, load_sems,
+    pad, pad_g, taps, normed, inv, lifted, gmix, glift, slope, gacts, order, gconv, kparts,
     grads, got1, send2, got2, kgrads, kgot1, ksend2, kgot2,
     emb, emb1, emb_sum, emb2, send3, got3, send4, half, other,
     edge_first, edge_last, north_g, south_g,
-    s_halo, r_halo, s1, r1, s1k, r1k, s2, r2, s2k, r2k, s_e, r_e, s3, r3, s4, r4, s5, r5,
+    s_fore, r_fore, s_halo, r_halo, s1, r1, s1k, r1k, s2, r2, s2k, r2k, s_e, r_e, s3, r3, s4, r4, s5, r5,
 ):
     dp, space = lax.axis_index("dp"), lax.axis_index("space")
     core = lax.rem(space, 2)
@@ -130,82 +123,114 @@
     after = (dp, lax.rem(space + 1, spaces))
 
     loads = {}
-    sources = (
-        (own_in, own), (north_in, north), (south_in, south), (ker_in, ker), (gain_in, gain),
-        (up_in, up), (cot_in, cot), (scale_in, scale), (w_in_in, w_in), (w_out_in, w_out),
+    sources = dict(
+        own=(own_in, own), ker=(ker_in, ker), up=(up_in, up), cot=(cot_in, cot),
+        scale=(scale_in, scale), w_out=(w_out_in, w_out), gain=(gain_in, gain), w_in=(w_in_in, w_in),
     )
-    for n, (src, dst) in enumerate(sources):
-        loads[n] = pltpu.make_async_copy(src, dst, load_sems.at[n])
-        loads[n].start()
-
-    greet(partner)
-    greet(before)
-    greet(after)
-
-    @pl.loop(1, 16)
-    def _(k):
-        greet(at(dp, plane, lax.rem(z + k, 16)))
-        greet(chunk_device(lax.rem(spot + k, 16)))
-
-    loads[3].wait()
-    load_taps(ker, taps)
-    for n in (0, 1, 2):
-        loads[n].wait()
+    for n, (name, (src, dst)) in enumerate(sources.items()):
+        loads[name] = pltpu.make_async_copy(src, dst, load_sems.at[n])
+        loads[name].start()
+
+    with scope("greet"):
+        greet(before)
+        greet(after)
+
+        @pl.loop(1, 16)
+        def _(k):
+            greet(at(dp, plane, lax.rem(z + k, 16)))
+            greet(chunk_device(lax.rem(spot + k, 16)))
+
+    with scope("gmix"):
+        for name in ("own", "up", "cot", "scale"):
+            loads[name].wait()
+        scale_row = scale[...].reshape(1, C)
+        emb_own = jnp.zeros((1, C), F32)
+        for t in range(CAP):
+            live = live_of(cnt, t)
+            here = slice(t * 64, t * 64 + 64)
+            g_out = grad_out_of(up, pw, cot, live, t)
+            gmix[here, :] = (g_out * scale_row[None]).astype(BF16).reshape(64, C)
+            weight = live * pw[0, t]
+            emb_own = emb_own + weight * jnp.sum(
+                own[t].astype(F32).reshape(64, C), axis=0, keepdims=True
+            )
+
+    with scope("barrier"):
+        pl.semaphore_wait(pltpu.get_barrier_semaphore(), 32)
+    down = copy_to(after, own.at[:, TILE - 3 :], north, s_fore.at[0], r_fore.at[0])
+    upward = copy_to(before, own.at[:, :3], south, s_fore.at[1], r_fore.at[1])
+    down.start()
+    upward.start()
 
     def groups_of(ref):
         return lambda i: split_groups(ref[i].astype(F32))
 
-    @pl.loop(0, CAP)
-    def _(t):
-        spread(adj, t, pad, groups_of(own), groups_of(north), groups_of(south))
-
-    @pl.loop(0, CAP)
-    def _(t):
-        @pl.loop(0, CG)
-        def _(g):
-            rows = conv_tile(pad, taps, g, t, False)
-            for a in range(TILE):
-                normed[g, t, a] = rows[a]
-
-    for n in (4, 5, 6, 7):
-        loads[n].wait()
-    emb_own = jnp.zeros((1, C), F32)
-    for t in range(CAP):
-        live = live_of(cnt, t)
-        x = [normed[g, t].reshape(64, 128) for g in range(CG)]
-        mean = jnp.sum(x[0] + x[1] + x[2], axis=-1, keepdims=True) / C
-        x = [v - mean for v in x]
-        var = jnp.sum(x[0] * x[0] + x[1] * x[1] + x[2] * x[2], axis=-1, keepdims=True) / C
-        istd = jnp.broadcast_to(lax.rsqrt(var + 1e-06), (64, 128))
-        inv[t] = istd
-        here = slice(t * 64, t * 64 + 64)
-        for g in range(CG):
-            lanes = slice(g * 128, g * 128 + 128)
-            n = x[g] * istd
-            normed[g, t] = n.reshape(TILE, TILE, 128)
-            lifted[here, lanes] = (n * gain[:, lanes]).astype(BF16)
-        g_out = grad_out_of(up, pw, cot, live, t)
-        gmix[here, :] = (g_out * scale[...][None]).astype(BF16).reshape(64, C)
-        weight = live * pw[0, t]
-        emb_own = emb_own + weight * jnp.sum(own[t].astype(F32).reshape(64, C), axis=0, keepdims=True)
-
-    d = lax.broadcasted_iota(jnp.int32, (8, CHUNK), 1)
-    d_core = jnp.where(d >= 192, 1, 0)
-    d = d - 192 * d_core
-    d_dp = jnp.zeros_like(d)
-    for m in range(1, 8):
-        d_dp = d_dp + jnp.where(d >= 24 * m, 1, 0)
-    d = d - 24 * d_dp
-    d_z = jnp.zeros_like(d)
-    for m in range(1, 8):
-        d_z = d_z + jnp.where(d >= 3 * m, 1, 0)
-    d = d - 3 * d_z
-    source = d_z * 48 + d_core * 24 + d_dp * 3 + d
-    rows = lax.broadcasted_iota(jnp.int32, (CHUNK, CHUNK), 0)
-    order = jnp.where(rows == source[0:1], 1.0, 0.0).astype(BF16)
-
-    loads[8].wait()
-    loads[9].wait()
+    with scope("under_halo"):
+        loads["ker"].wait()
+        load_taps(ker, taps)
+
+        @pl.loop(0, CAP)
+        def _(t):
+            spread(adj, t, pad, groups_of(own), None, None)
+
+        d = lax.broadcasted_iota(jnp.int32, (8, CHUNK), 1)
+        d_core = jnp.where(d >= 192, 1, 0)
+        d = d - 192 * d_core
+        d_dp = jnp.zeros_like(d)
+        for m in range(1, 8):
+            d_dp = d_dp + jnp.where(d >= 24 * m, 1, 0)
+        d = d - 24 * d_dp
+        d_z = jnp.zeros_like(d)
+        for m in range(1, 8):
+            d_z = d_z + jnp.where(d >= 3 * m, 1, 0)
+        d = d - 3 * d_z
+        source = d_z * 48 + d_core * 24 + d_dp * 3 + d
+        rows = lax.broadcasted_iota(jnp.int32, (CHUNK, CHUNK), 0)
+        order[...] = jnp.where(rows == source[0:1], 1.0, 0.0).astype(BF16)
+        loads["w_out"].wait()
+        for h in range(HID // CHUNK):
+            here = slice(h * CHUNK, (h + 1) * CHUNK)
+            gacts[:, here] = lax.dot_general(
+                gmix[...], w_out[here, :], (((1,), (1,)), ((), ())), preferred_element_type=F32
+            )
+
+    with scope("halo_wait"):
+        down.wait_recv()
+        upward.wait_recv()
+
+    with scope("spread"):
+
+        @pl.loop(0, CAP)
+        def _(t):
+            spread(adj, t, pad, None, groups_of(north), groups_of(south))
+
+    with scope("conv"):
+
+        @pl.loop(0, CAP)
+        def _(t):
+            @pl.loop(0, CG)
+            def _(g):
+                rows = conv_tile(pad, taps, g, t, False)
+                for a in range(TILE):
+                    normed[g, t, a] = rows[a]
+
+    with scope("norm"):
+        loads["gain"].wait()
+        gain_row = gain[...].reshape(1, C)
+        for t in range(CAP):
+            x = [normed[g, t].reshape(64, 128) for g in range(CG)]
+            mean = jnp.sum(x[0] + x[1] + x[2], axis=-1, keepdims=True) / C
+            x = [v - mean for v in x]
+            var = jnp.sum(x[0] * x[0] + x[1] * x[1] + x[2] * x[2], axis=-1, keepdims=True) / C
+            istd = jnp.broadcast_to(lax.rsqrt(var + 1e-06), (64, 128))
+            inv[t] = istd
+            here = slice(t * 64, t * 64 + 64)
+            for g in range(CG):
+                lanes = slice(g * 128, g * 128 + 128)
+                n = x[g] * istd
+                normed[g, t] = n.reshape(TILE, TILE, 128)
+                lifted[here, lanes] = (n * gain_row[:, lanes]).astype(BF16)
+        loads["w_in"].wait()
 
     def pair_of(h):
         return copy_to(partner, grads.at[1 - core, h], got1.at[h], s1.at[h], r1.at[h])
@@ -241,15 +266,13 @@
         act = (pre * cdf).astype(BF16)
         density = jnp.exp(-0.5 * pre * pre) * inv_root_two_pi
         slope[:, here] = cdf + pre * density
-        sent = jnp.dot(act, order, preferred_element_type=F32).astype(BF16)
+        sent = jnp.dot(act, order[...], preferred_element_type=F32).astype(BF16)
         gw = lax.dot_general(
             sent, gmix[...], (((0,), (0,)), ((), ())), preferred_element_type=F32
         ).astype(BF16)
         for c in range(2):
             for m in range(8):
                 grads[c, h, m] = gw[(c * 8 + m) * 24 : (c * 8 + m) * 24 + 24]
-        if h == 0:
-            pl.semaphore_wait(pltpu.get_barrier_semaphore(), 33)
         pair_of(h).start()
         pooled = jnp.zeros((1, CHUNK), F32)
         for t in range(CAP):
@@ -266,16 +289,13 @@
         if h > 0:
             pass_on(h - 1)
     mix = jnp.sum(mixed, axis=0, keepdims=True)
-    emb[...] = jnp.broadcast_to((emb_own + scale[...] * mix) / TILE, (8, C))
+    emb[...] = jnp.broadcast_to((emb_own + scale_row * mix) / TILE, (8, C))
     emb_pair = copy_to(partner, emb, emb1, s_e.at[0], r_e.at[0])
     emb_pair.start()
 
     for h in range(HID // CHUNK):
         here = slice(h * CHUNK, (h + 1) * CHUNK)
-        gact = lax.dot_general(
-            gmix[...], w_out[here, :], (((1,), (1,)), ((), ())), preferred_element_type=F32
-        )
-        gpre = (gact * slope[:, here]).astype(BF16)
+        gpre = (gacts[:, here] * slope[:, here]).astype(BF16)
         gl = lax.dot_general(
             gpre, w_in[:, here], (((1,), (1,)), ((), ())), preferred_element_type=F32
         )
@@ -287,7 +307,7 @@
 
     for t in range(CAP):
         here = slice(t * 64, t * 64 + 64)
-        gn = [glift[here, g * 128 : g * 128 + 128] * gain[:, g * 128 : g * 128 + 128] for g in range(CG)]
+        gn = [glift[here, g * 128 : g * 128 + 128] * gain_row[:, g * 128 : g * 128 + 128] for g in range(CG)]
         n = [normed[g, t].reshape(64, 128) for g in range(CG)]
         m1 = jnp.sum(gn[0] + gn[1] + gn[2], axis=-1, keepdims=True) / C
         m2 = jnp.sum(gn[0] * n[0] + gn[1] * n[1] + gn[2] * n[2], axis=-1, keepdims=True) / C
@@ -374,6 +394,10 @@
 
             kgot2[spot] = ksend2[spot]
 
+    out_copy = pltpu.make_async_copy(out, out_hbm, out_sems.at[0])
+    out_copy.start()
+    down.wait_send()
+    upward.wait_send()
     across.wait_recv()
     emb_both = emb_sum[0:1] + emb2[0:1]
     high = emb_both.astype(BF16).astype(F32)
@@ -447,7 +471,8 @@
 
     swap = copy_to(partner, half, other, s5.at[0], r5.at[0])
     swap.start()
-    got4[spot] = send4[...]
+    own_copy = pltpu.make_async_copy(send4, got4.at[spot], out_sems.at[1])
+    own_copy.start()
 
     @pl.loop(1, 16)
     def _(k):
@@ -456,6 +481,11 @@
 
     swap.wait()
     emb_out[...] = half[...] + other[...]
+    emb_copy = pltpu.make_async_copy(emb_out, emb_hbm, out_sems.at[2])
+    emb_copy.start()
+    out_copy.wait()
+    own_copy.wait()
+    emb_copy.wait()
 
     @pl.loop(1, 16)
     def _(k):
@@ -463,15 +493,24 @@
         last(q, q, k).wait()
 
 
-def finish_kernel(out, got4, emb_got, emb, tiles, w_grad, k_grad):
+def finish_kernel(out, got4_in, emb_in, emb, tiles, w_grad, k_grad, got4, emb_got, sems):
     plane = lax.axis_index("space") // 32
-    tiles[...] = out[...]
-    emb[...] = emb_got[0:1]
+    loads = [
+        pltpu.make_async_copy(got4_in, got4, sems.at[0]),
+        pltpu.make_async_copy(emb_in, emb_got, sems.at[1]),
+        pltpu.make_async_copy(out, tiles, sems.at[2]),
+    ]
+    for load in loads:
+        load.start()
+    loads[0].wait()
     for d in range(8):
         w_grad[d * 3 : d * 3 + 3, :] = got4[d * 2 + plane, 0:3].astype(F32)
     for ij in range(49):
         row = got4[ij // 4, 3 + ij % 4 : 4 + ij % 4].astype(F32)
         k_grad[ij // 7, ij % 7 : ij % 7 + 1, :] = row
+    loads[1].wait()
+    emb[...] = emb_got[0:1]
+    loads[2].wait()
 
 
 VMEM = pl.BlockSpec(memory_space=pltpu.VMEM)
@@ -496,16 +535,6 @@
     blocks = (CG, CAP, TILE, TILE, 128)
     chunks = HID // CHUNK
 
-    north, south = pl.pallas_call(
-        functools.partial(halo_kernel, spaces),
-        out_shape=(struct(halo, BF16), struct(halo, BF16)),
-        in_specs=[HBM],
-        out_specs=(HBM, HBM),
-        scratch_shapes=[dma((2,)), dma((2,))],
-        compiler_params=pltpu.CompilerParams(collective_id=0, has_side_effects=True),
-        name="halo",
-    )(own)
-
     out, got4, emb = pl.pallas_call(
         functools.partial(main_kernel, spaces),
         out_shape=(
@@ -513,20 +542,23 @@
             struct((16, 8, C), BF16),
             struct((8, C), F32),
         ),
-        in_specs=[SMEM] * 3 + [HBM] * 10,
-        out_specs=(VMEM,) * 3,
+        in_specs=[SMEM] * 3 + [HBM] * 8,
+        out_specs=(HBM,) * 3,
         scratch_shapes=[
+            vmem((CAP, TILE, TILE, C), BF16),
+            vmem((8, C), F32),
+            dma((3,)),
             vmem((CAP, TILE, TILE, C), BF16),
             vmem(halo, BF16),
             vmem(halo, BF16),
             vmem((CAP, TILE, TILE, C), BF16),
             vmem((1, C), F32),
             vmem((7, 7, C), F32),
-            vmem((1, C), F32),
-            vmem((1, C), F32),
+            vmem((C,), F32),
+            vmem((C,), F32),
             vmem((C, HID), BF16),
             vmem((HID, C), BF16),
-            dma((10,)),
+            dma((8,)),
             vmem((CG, CAP, 14, 24, 128), F32),
             vmem((CG, CAP, 14, 24, 128), F32),
             vmem((CG, 49, 8, 128), F32),
@@ -536,6 +568,8 @@
             vmem((PIX, C), BF16),
             vmem((PIX, C), F32),
             vmem((PIX, HID), F32),
+            vmem((PIX, HID), F32),
+            vmem((CHUNK, CHUNK), BF16),
             vmem(blocks, F32),
             vmem((CG, 49, 8, 128), F32),
             vmem((2, chunks, 8, 24, C), BF16),
@@ -560,6 +594,7 @@
             vmem(edge, BF16),
             vmem(edge, BF16),
             dma((2,)), dma((2,)),
+            dma((2,)), dma((2,)),
             dma((chunks,)), dma((chunks,)),
             dma((1,)), dma((1,)),
             dma((chunks, 8)), dma((16, 2)),
@@ -570,12 +605,12 @@
             dma((1,)), dma((1,)),
         ],
         compiler_params=pltpu.CompilerParams(
-            collective_id=1, has_side_effects=True, vmem_limit_bytes=48 << 20
+            collective_id=0, has_side_effects=True, vmem_limit_bytes=VMEM_BYTES
         ),
         name="main",
     )(
-        pool_weight, adjacency[0], counts, own, north, south, up, slide_cot, kernel,
-        norm_gain[None], layer_scale[None], w_in, w_out,
+        pool_weight, adjacency[0], counts, own, up, slide_cot, kernel, norm_gain, layer_scale, w_in,
+        w_out,
     )
 
     embedding, grad_tiles, w_grad, k_grad = pl.pallas_call(
@@ -586,8 +621,9 @@
             struct((24, C), F32),
             struct((7, 7, C), F32),
         ),
-        in_specs=[VMEM] * 3,
-        out_specs=(VMEM,) * 4,
+        in_specs=[HBM] * 3,
+        out_specs=(VMEM, HBM, VMEM, VMEM),
+        scratch_shapes=[vmem((16, 8, C), BF16), vmem((8, C), F32), dma((3,))],
         name="finish",
     )(out, got4, emb)
     return embedding, grad_tiles[None], w_grad, k_grad

time: 70.2 us -> 61.5 us (0.88)
  local copies, waits for them, and re-layouts: 12.3 us -> 0 us
  Pallas kernels: 56 us -> 59.9 us
    pallas_call x1 -> x0, Pallas kernels: 12.9 us -> none  [per_device(): pl.pallas_call(functools.partial(halo_kernel, spaces), out_shape=(struct(...]
    unnamed x26 -> x0, local copies, waits for them, and re-layouts: 11 us -> none
    pallas_call x1, Pallas kernels: 41.4 us -> 52.2 us  [per_device(): pl.pallas_call(functools.partial(main_kernel, spaces), out_shape=(struct(...]
    pallas_call x1, Pallas kernels: 1.73 us -> 7.74 us  [per_device(): pl.pallas_call(finish_kernel, out_shape=(struct((1, C), F32), struct((CAP...]
    broadcast_in_dim x2 -> x0, local copies, waits for them, and re-layouts: 1.37 us -> none  [the longest x1 0.68 us: per_device(): norm_gain[None]]
where the time goes in v3:
time: 61.5 us; the launch traced here: 61.2 us
  Pallas kernels  59.9 us (97%)
  between operations  1.29 us (2%)
    pallas_call x1, Pallas kernels, per_device(): pl.pallas_call(functools.partial(main_kernel, spaces), out_shape=(struct(...  52.2 us
    pallas_call x1, Pallas kernels, per_device(): pl.pallas_call(finish_kernel, out_shape=(struct((1, C), F32), struct((CAP...  7.74 us

profile of v3, /device:TPU:24, one launch (start us, length us, event | category | flops | bytes accessed | tf_op | source)
XLA Modules:
  0.0 61.2 jit_solution(6298655604074180392)
XLA Ops:
  1.3 52.2 %main.1 = (bf16[4,8,8,384]{3,2,1,0:T(8,128)(2,1)}, bf16[16,8,384]{2,1,0:T(8,128)(2,1)}, f32[8,384]{1,0:T(8,128)}) custom-call(f32[1,4]{1,0:T(1,128)} %pw.1, s32[4,8]{1,0:T(4,128)} %bitcast.6, s32[1,1]{1,0:T(1,128)S(6)} %copy.15.cnt, bf16[4,8,8,384]{3,2,1,0:T(8,128)(2,1)} %bitcast.4, bf16[4,8,8,384]{3,2,1,0:T(8,128)(2,1)} %bitcast.5, f32[1,384]{1,0:T(1,128)} %cot_in.1, ...), custom_call_target="tpu_custom_call" | custom-call | tf_op jit(solution)/shard_map/main/pallas_call | solution.py:538
  53.5 7.7 %finish.1 = (f32[1,384]{1,0:T(1,128)}, bf16[4,8,8,384]{3,2,1,0:T(8,128)(2,1)}, f32[24,384]{1,0:T(8,128)}, f32[7,7,384]{2,1,0:T(8,128)}) custom-call(bf16[4,8,8,384]{3,2,1,0:T(8,128)(2,1)} %get-tuple-element.11.out, bf16[16,8,384]{2,1,0:T(8,128)(2,1)} %get-tuple-element.12.got4_in, f32[8,384]{1,0:T(8,128)} %get-tuple-element.13.emb_in), custom_call_target="tpu_custom_call" | custom-call | tf_op jit(solution)/shard_map/finish/pallas_call | solution.py:616

commit v4 on v3

--- a/solution.py
+++ b/solution.py
@@ -47,11 +47,11 @@
                 pad[g, t, row : row + rows, 8 * place : 8 * place + 8, :] = groups[g]
 
 
-def conv_tile(pad, taps, g, t, flip):
-    total = [None] * TILE
+def conv_tile(pad, taps, g, t, flip, rows=range(14), start=None):
+    total = list(start) if start is not None else [None] * TILE
     for j in range(7):
         column = [taps[g, 48 - (i * 7 + j) if flip else i * 7 + j] for i in range(7)]
-        for r in range(14):
+        for r in rows:
             window = pad[g, t, r, 5 + j : 13 + j, :]
             for i in range(7):
                 a = r - i
@@ -59,6 +59,20 @@
                     term = window * column[i]
                     total[a] = term if total[a] is None else total[a] + term
     return total
+
+
+OWN_ROWS = range(3, 11)
+EDGE_ROWS = (0, 1, 2, 11, 12, 13)
+RING_ORDER = (8, 7, 9, 6, 10, 5, 11, 4, 12, 3, 13, 2, 14, 1, 15)
+PLANE_ORDER = (
+    (2, 2), (2, 1), (2, 3), (1, 2), (3, 2), (2, 0), (0, 2), (1, 1), (1, 3), (3, 1), (3, 3), (0, 1),
+    (0, 3), (1, 0), (3, 0),
+)
+DP_ORDER = (4, 5, 3, 2, 6, 7, 1)
+
+
+def wrapped(value, size):
+    return jnp.where(value >= size, value - size, value)
 
 
 def split_groups(value):
@@ -115,8 +129,11 @@
     def at(d, p, zz):
         return (d, (p * 16 + zz) * 2 + core)
 
-    def chunk_device(q):
-        return at(q // 2, lax.rem(q, 2), z)
+    px, py = dp // 2, lax.rem(dp, 2) * 2 + plane
+
+    def plane_device(dx, dy):
+        x, y = wrapped(px + dx, 4), wrapped(py + dy, 4)
+        return x * 4 + y, at(x * 2 + y // 2, lax.rem(y, 2), z)
 
     partner = (dp, space + 1 - 2 * core)
     before = (dp, lax.rem(space + spaces - 1, spaces))
@@ -135,10 +152,10 @@
         greet(before)
         greet(after)
 
-        @pl.loop(1, 16)
-        def _(k):
-            greet(at(dp, plane, lax.rem(z + k, 16)))
-            greet(chunk_device(lax.rem(spot + k, 16)))
+        for k in RING_ORDER:
+            greet(at(dp, plane, wrapped(z + k, 16)))
+        for dx, dy in PLANE_ORDER:
+            greet(plane_device(dx, dy)[1])
 
     with scope("gmix"):
         for name in ("own", "up", "cot", "scale"):
@@ -188,6 +205,15 @@
         rows = lax.broadcasted_iota(jnp.int32, (CHUNK, CHUNK), 0)
         order[...] = jnp.where(rows == source[0:1], 1.0, 0.0).astype(BF16)
         loads["w_out"].wait()
+
+        @pl.loop(0, CAP)
+        def _(t):
+            @pl.loop(0, CG)
+            def _(g):
+                rows = conv_tile(pad, taps, g, t, False, OWN_ROWS)
+                for a in range(TILE):
+                    normed[g, t, a] = rows[a]
+
         for h in range(HID // CHUNK):
             here = slice(h * CHUNK, (h + 1) * CHUNK)
             gacts[:, here] = lax.dot_general(
@@ -210,7 +236,8 @@
         def _(t):
             @pl.loop(0, CG)
             def _(g):
-                rows = conv_tile(pad, taps, g, t, False)
+                start = [normed[g, t, a] for a in range(TILE)]
+                rows = conv_tile(pad, taps, g, t, False, EDGE_ROWS, start)
                 for a in range(TILE):
                     normed[g, t, a] = rows[a]
 
@@ -236,7 +263,7 @@
         return copy_to(partner, grads.at[1 - core, h], got1.at[h], s1.at[h], r1.at[h])
 
     def plane_of(h, k):
-        to = lax.rem(dp + k, 8)
+        to = wrapped(dp + k, 8)
         return copy_to(
             at(to, h // 2, z), send2.at[h, to], got2.at[spot, h % 2], s2.at[h, k],
             r2.at[spot, h % 2],
@@ -246,8 +273,7 @@
         pair_of(h).wait_recv()
         send2[h] = (grads[core, h].astype(F32) + got1[h].astype(F32)).astype(BF16)
 
-        @pl.loop(1, 8)
-        def _(k):
+        for k in DP_ORDER:
             plane_of(h, k).start()
 
         @pl.when(plane == h // 2)
@@ -362,8 +388,27 @@
     def from_edge(ref):
         return lambda i: [ref[g, i].astype(F32) for g in range(CG)]
 
-    def back(t):
-        spread(adj, t, pad_g, from_tiles, from_edge(north_g), from_edge(south_g))
+    @pl.loop(0, CAP)
+    def _(t):
+        spread(adj, t, pad_g, from_tiles, None, None)
+
+    def kplane(n, arriving=False):
+        q, device = plane_device(*PLANE_ORDER[n])
+        slot = q if arriving else spot
+        return copy_to(device, ksend2.at[q], kgot2.at[slot], s2k.at[n], r2k.at[slot])
+
+    kpair.wait_recv()
+    ksend2[...] = (kgrads[...].astype(F32) + kgot1[...].astype(F32)).astype(BF16)
+    for n in range(15):
+        kplane(n).start()
+    kgot2[spot] = ksend2[spot]
+
+    to_after.wait_recv()
+    to_before.wait_recv()
+
+    @pl.loop(0, CAP)
+    def _(t):
+        spread(adj, t, pad_g, None, from_edge(north_g), from_edge(south_g))
         live = live_of(cnt, t)
         for g in range(CG):
             lanes = slice(g * 128, g * 128 + 128)
@@ -372,27 +417,6 @@
             for a in range(TILE):
                 g_out = live * (up[t, a, :, lanes].astype(F32) + extra)
                 out[t, a, :, lanes] = (live * (g_out + rows[a])).astype(BF16)
-
-    to_after.wait_recv()
-    to_before.wait_recv()
-
-    def kplane(q, slot, k):
-        return copy_to(chunk_device(q), ksend2.at[q], kgot2.at[slot], s2k.at[k], r2k.at[slot])
-
-    @pl.loop(0, CAP)
-    def _(t):
-        back(t)
-
-        @pl.when(t == 0)
-        def _():
-            kpair.wait_recv()
-            ksend2[...] = (kgrads[...].astype(F32) + kgot1[...].astype(F32)).astype(BF16)
-
-            @pl.loop(1, 16)
-            def _(k):
-                kplane(lax.rem(spot + k, 16), spot, k).start()
-
-            kgot2[spot] = ksend2[spot]
 
     out_copy = pltpu.make_async_copy(out, out_hbm, out_sems.at[0])
     out_copy.start()
@@ -409,12 +433,11 @@
     to_after.wait_send()
     to_before.wait_send()
 
-    @pl.loop(1, 16)
-    def _(k):
-        q = lax.rem(spot + k, 16)
-        kplane(q, q, k).wait_recv()
+    for n in range(15):
+        kplane(n, True).wait_recv()
+        q, device = plane_device(*PLANE_ORDER[n])
         for hh in range(2):
-            copy_to(partner, send2.at[0, 0], got2.at[q, hh], s2.at[0, 0], r2.at[q, hh]).wait_recv()
+            copy_to(device, send2.at[0, 0], got2.at[q, hh], s2.at[0, 0], r2.at[q, hh]).wait_recv()
 
     total = [got2[0, hh].astype(F32) for hh in range(2)]
     tail = kgot2[0].astype(F32)
@@ -426,34 +449,29 @@
         row = q % 8 * 3
         send3[q] = jnp.concatenate([total[q // 8][row : row + 3], tail, mine], axis=0).astype(BF16)
 
-    def ring(q, slot, k):
+    def ring(k, arriving=False):
+        q = wrapped(z + k, 16)
+        slot = q if arriving else z
         return copy_to(at(dp, plane, q), send3.at[q], got3.at[slot], s3.at[k], r3.at[slot])
 
-    @pl.loop(1, 16)
-    def _(k):
-        ring(lax.rem(z + k, 16), z, k).start()
+    for k in RING_ORDER:
+        ring(k).start()
 
     got3[z] = send3[z]
     across.wait_send()
     for h in range(HID // CHUNK):
 
-        @pl.loop(1, 8)
-        def _(k):
+        for k in DP_ORDER:
             plane_of(h, k).wait_send()
 
         @pl.when(plane != h // 2)
         def _():
             plane_of(h, 0).wait_send()
 
-    @pl.loop(1, 16)
-    def _(k):
-        q = lax.rem(spot + k, 16)
-        kplane(q, q, k).wait_send()
-
-    @pl.loop(1, 16)
-    def _(k):
-        q = lax.rem(z + k, 16)
-        ring(q, q, k).wait_recv()
+    for n in range(15):
+        kplane(n).wait_send()
+    for k in RING_ORDER:
+        ring(k, True).wait_recv()
 
     total = got3[0].astype(F32)
     for q in range(1, 16):
@@ -462,22 +480,21 @@
     send4[...] = total.astype(BF16)
     half[...] = jnp.broadcast_to(total[7:8], (8, C))
 
-    def last(q, slot, k):
-        return copy_to(chunk_device(q), send4, got4.at[slot], s4.at[k], r4.at[slot])
-
-    @pl.loop(1, 16)
-    def _(k):
-        last(lax.rem(spot + k, 16), spot, k).start()
+    def last(n, arriving=False):
+        q, device = plane_device(*PLANE_ORDER[n])
+        slot = q if arriving else spot
+        return copy_to(device, send4, got4.at[slot], s4.at[n], r4.at[slot])
+
+    for n in range(15):
+        last(n).start()
 
     swap = copy_to(partner, half, other, s5.at[0], r5.at[0])
     swap.start()
     own_copy = pltpu.make_async_copy(send4, got4.at[spot], out_sems.at[1])
     own_copy.start()
 
-    @pl.loop(1, 16)
-    def _(k):
-        q = lax.rem(z + k, 16)
-        ring(q, q, k).wait_send()
+    for k in RING_ORDER:
+        ring(k).wait_send()
 
     swap.wait()
     emb_out[...] = half[...] + other[...]
@@ -487,10 +504,10 @@
     own_copy.wait()
     emb_copy.wait()
 
-    @pl.loop(1, 16)
-    def _(k):
-        q = lax.rem(spot + k, 16)
-        last(q, q, k).wait()
+    for n in range(15):
+        last(n, True).wait_recv()
+    for n in range(15):
+        last(n).wait_send()
 
 
 def finish_kernel(out, got4_in, emb_in, emb, tiles, w_grad, k_grad, got4, emb_got, sems):
@@ -622,7 +639,7 @@
             struct((7, 7, C), F32),
         ),
         in_specs=[HBM] * 3,
-        out_specs=(VMEM, HBM, VMEM, VMEM),
+        out_specs=(VMEM,) * 4,
         scratch_shapes=[vmem((16, 8, C), BF16), vmem((8, C), F32), dma((3,))],
         name="finish",
     )(out, got4, emb)

time: 61.5 us -> 51.3 us (0.83)
  Pallas kernels: 59.9 us -> 49.7 us
    pallas_call x1, Pallas kernels: 7.74 us -> 1.74 us  [per_device(): pl.pallas_call(finish_kernel, out_shape=(struct((1, C), F32), struct((CAP...]
    pallas_call x1, Pallas kernels: 52.2 us -> 47.9 us  [per_device(): pl.pallas_call(functools.partial(main_kernel, spaces), out_shape=(struct(...]
where the time goes in v4:
time: 51.3 us; the launch traced here: 51 us
  Pallas kernels  49.7 us (97%)
  between operations  1.29 us (3%)
    pallas_call x1, Pallas kernels, per_device(): pl.pallas_call(functools.partial(main_kernel, spaces), out_shape=(struct(...  47.9 us
    pallas_call x1, Pallas kernels, per_device(): pl.pallas_call(finish_kernel, out_shape=(struct((1, C), F32), struct((CAP...  1.74 us

profile of v4, /device:TPU:24, one launch (start us, length us, event | category | flops | bytes accessed | tf_op | source)
XLA Modules:
  0.0 51.0 jit_solution(11252904346260860308)
XLA Ops:
  1.3 47.9 %main.1 = (bf16[4,8,8,384]{3,2,1,0:T(8,128)(2,1)}, bf16[16,8,384]{2,1,0:T(8,128)(2,1)}, f32[8,384]{1,0:T(8,128)}) custom-call(f32[1,4]{1,0:T(1,128)} %pw.1, s32[4,8]{1,0:T(4,128)} %bitcast.6, s32[1,1]{1,0:T(1,128)S(6)} %copy.15.cnt, bf16[4,8,8,384]{3,2,1,0:T(8,128)(2,1)} %bitcast.4, bf16[4,8,8,384]{3,2,1,0:T(8,128)(2,1)} %bitcast.5, f32[1,384]{1,0:T(1,128)} %cot_in.1, ...), custom_call_target="tpu_custom_call" | custom-call | tf_op jit(solution)/shard_map/main/pallas_call | solution.py:555
  49.2 1.7 %finish.1 = (f32[1,384]{1,0:T(1,128)}, bf16[4,8,8,384]{3,2,1,0:T(8,128)(2,1)}, f32[24,384]{1,0:T(8,128)}, f32[7,7,384]{2,1,0:T(8,128)}) custom-call(bf16[4,8,8,384]{3,2,1,0:T(8,128)(2,1)} %get-tuple-element.11.out, bf16[16,8,384]{2,1,0:T(8,128)(2,1)} %get-tuple-element.12.got4_in, f32[8,384]{1,0:T(8,128)} %get-tuple-element.13.emb_in), custom_call_target="tpu_custom_call" | custom-call | tf_op jit(solution)/shard_map/finish/pallas_call | solution.py:633

commit v5 on v4

--- a/solution.py
+++ b/solution.py
@@ -118,7 +118,7 @@
     grads, got1, send2, got2, kgrads, kgot1, ksend2, kgot2,
     emb, emb1, emb_sum, emb2, send3, got3, send4, half, other,
     edge_first, edge_last, north_g, south_g,
-    s_fore, r_fore, s_halo, r_halo, s1, r1, s1k, r1k, s2, r2, s2k, r2k, s_e, r_e, s3, r3, s4, r4, s5, r5,
+    heard, s_fore, r_fore, s_halo, r_halo, s1, r1, s1k, r1k, s2, r2, s2k, r2k, s_e, r_e, s3, r3, s4, r4, s5, r5,
 ):
     dp, space = lax.axis_index("dp"), lax.axis_index("space")
     core = lax.rem(space, 2)
@@ -152,10 +152,11 @@
         greet(before)
         greet(after)
 
-        for k in RING_ORDER:
+        for k in (2, 14, 1, 15):
             greet(at(dp, plane, wrapped(z + k, 16)))
-        for dx, dy in PLANE_ORDER:
-            greet(plane_device(dx, dy)[1])
+        for d in (2, 1, 3):
+            greet(plane_device(d, 0)[1])
+            greet(plane_device(0, d)[1])
 
     with scope("gmix"):
         for name in ("own", "up", "cot", "scale"):
@@ -173,11 +174,19 @@
             )
 
     with scope("barrier"):
-        pl.semaphore_wait(pltpu.get_barrier_semaphore(), 32)
+        pl.semaphore_wait(pltpu.get_barrier_semaphore(), 12)
+
+    def tell(device, sem):
+        pl.semaphore_signal(sem, inc=1, device_id=device, device_id_type=MESH)
+
     down = copy_to(after, own.at[:, TILE - 3 :], north, s_fore.at[0], r_fore.at[0])
     upward = copy_to(before, own.at[:, :3], south, s_fore.at[1], r_fore.at[1])
     down.start()
     upward.start()
+    for d in (2, 1, 3):
+        tell(plane_device(d, 0)[1], heard.at[0])
+    for k in (2, 14):
+        tell(at(dp, plane, wrapped(z + k, 16)), heard.at[1])
 
     def groups_of(ref):
         return lambda i: split_groups(ref[i].astype(F32))
@@ -240,6 +249,11 @@
                 rows = conv_tile(pad, taps, g, t, False, EDGE_ROWS, start)
                 for a in range(TILE):
                     normed[g, t, a] = rows[a]
+
+    pl.semaphore_wait(heard.at[0], 3)
+    pl.semaphore_wait(heard.at[1], 2)
+    for k in (4, 12):
+        tell(at(dp, plane, wrapped(z + k, 16)), heard.at[2])
 
     with scope("norm"):
         loads["gain"].wait()
@@ -444,6 +458,8 @@
     for q in range(1, 16):
         total = [total[hh] + got2[q, hh].astype(F32) for hh in range(2)]
         tail = tail + kgot2[q].astype(F32)
+
+    pl.semaphore_wait(heard.at[2], 2)
 
     for q in range(16):
         row = q % 8 * 3
@@ -610,6 +626,7 @@
             vmem(edge, BF16),
             vmem(edge, BF16),
             vmem(edge, BF16),
+            pltpu.SemaphoreType.REGULAR((3,)),
             dma((2,)), dma((2,)),
             dma((2,)), dma((2,)),
             dma((chunks,)), dma((chunks,)),

time: 51.3 us -> 49.5 us (0.965); the launches traced: 51 us -> 48.6 us
  Pallas kernels: 49.7 us -> 47.3 us
    pallas_call x1, Pallas kernels: 47.9 us -> 45.5 us  [per_device(): pl.pallas_call(functools.partial(main_kernel, spaces), out_shape=(struct(...]
where the time goes in v5:
time: 49.5 us; the launch traced here: 48.6 us
  Pallas kernels  47.3 us (96%)
  between operations  1.29 us (3%)
    pallas_call x1, Pallas kernels, per_device(): pl.pallas_call(functools.partial(main_kernel, spaces), out_shape=(struct(...  45.5 us
    pallas_call x1, Pallas kernels, per_device(): pl.pallas_call(finish_kernel, out_shape=(struct((1, C), F32), struct((CAP...  1.74 us

profile of v5, /device:TPU:24, one launch (start us, length us, event | category | flops | bytes accessed | tf_op | source)
XLA Modules:
  0.0 48.6 jit_solution(3904290004416116720)
XLA Ops:
  1.3 45.5 %main.1 = (bf16[4,8,8,384]{3,2,1,0:T(8,128)(2,1)}, bf16[16,8,384]{2,1,0:T(8,128)(2,1)}, f32[8,384]{1,0:T(8,128)}) custom-call(f32[1,4]{1,0:T(1,128)} %pw.1, s32[4,8]{1,0:T(4,128)} %bitcast.6, s32[1,1]{1,0:T(1,128)S(6)} %copy.15.cnt, bf16[4,8,8,384]{3,2,1,0:T(8,128)(2,1)} %bitcast.4, bf16[4,8,8,384]{3,2,1,0:T(8,128)(2,1)} %bitcast.5, f32[1,384]{1,0:T(1,128)} %cot_in.1, ...), custom_call_target="tpu_custom_call" | custom-call | tf_op jit(solution)/shard_map/main/pallas_call | solution.py:571
  46.8 1.7 %finish.1 = (f32[1,384]{1,0:T(1,128)}, bf16[4,8,8,384]{3,2,1,0:T(8,128)(2,1)}, f32[24,384]{1,0:T(8,128)}, f32[7,7,384]{2,1,0:T(8,128)}) custom-call(bf16[4,8,8,384]{3,2,1,0:T(8,128)(2,1)} %get-tuple-element.11.out, bf16[16,8,384]{2,1,0:T(8,128)(2,1)} %get-tuple-element.12.got4_in, f32[8,384]{1,0:T(8,128)} %get-tuple-element.13.emb_in), custom_call_target="tpu_custom_call" | custom-call | tf_op jit(solution)/shard_map/finish/pallas_call | solution.py:650

commit v6 on v5

--- a/solution.py
+++ b/solution.py
@@ -158,8 +158,24 @@
             greet(plane_device(d, 0)[1])
             greet(plane_device(0, d)[1])
 
+    with scope("barrier"):
+        pl.semaphore_wait(pltpu.get_barrier_semaphore(), 12)
+
+    def tell(device, sem):
+        pl.semaphore_signal(sem, inc=1, device_id=device, device_id_type=MESH)
+
+    loads["own"].wait()
+    down = copy_to(after, own.at[:, TILE - 3 :], north, s_fore.at[0], r_fore.at[0])
+    upward = copy_to(before, own.at[:, :3], south, s_fore.at[1], r_fore.at[1])
+    down.start()
+    upward.start()
+    for d in (2, 1, 3):
+        tell(plane_device(d, 0)[1], heard.at[0])
+    for k in (2, 14):
+        tell(at(dp, plane, wrapped(z + k, 16)), heard.at[1])
+
     with scope("gmix"):
-        for name in ("own", "up", "cot", "scale"):
+        for name in ("up", "cot", "scale"):
             loads[name].wait()
         scale_row = scale[...].reshape(1, C)
         emb_own = jnp.zeros((1, C), F32)
@@ -172,21 +188,6 @@
             emb_own = emb_own + weight * jnp.sum(
                 own[t].astype(F32).reshape(64, C), axis=0, keepdims=True
             )
-
-    with scope("barrier"):
-        pl.semaphore_wait(pltpu.get_barrier_semaphore(), 12)
-
-    def tell(device, sem):
-        pl.semaphore_signal(sem, inc=1, device_id=device, device_id_type=MESH)
-
-    down = copy_to(after, own.at[:, TILE - 3 :], north, s_fore.at[0], r_fore.at[0])
-    upward = copy_to(before, own.at[:, :3], south, s_fore.at[1], r_fore.at[1])
-    down.start()
-    upward.start()
-    for d in (2, 1, 3):
-        tell(plane_device(d, 0)[1], heard.at[0])
-    for k in (2, 14):
-        tell(at(dp, plane, wrapped(z + k, 16)), heard.at[1])
 
     def groups_of(ref):
         return lambda i: split_groups(ref[i].astype(F32))

time: 49.5 us -> 49.3 us (level)
  no operation moved by 1% of the time
where the time goes in v6:
time: 49.3 us; the launch traced here: 48.6 us
  Pallas kernels  47.3 us (96%)
  between operations  1.29 us (3%)
    pallas_call x1, Pallas kernels, per_device(): pl.pallas_call(functools.partial(main_kernel, spaces), out_shape=(struct(...  45.6 us
    pallas_call x1, Pallas kernels, per_device(): pl.pallas_call(finish_kernel, out_shape=(struct((1, C), F32), struct((CAP...  1.74 us

profile of v6, /device:TPU:24, one launch (start us, length us, event | category | flops | bytes accessed | tf_op | source)
XLA Modules:
  0.0 48.6 jit_solution(7280762576685517007)
XLA Ops:
  1.3 45.6 %main.1 = (bf16[4,8,8,384]{3,2,1,0:T(8,128)(2,1)}, bf16[16,8,384]{2,1,0:T(8,128)(2,1)}, f32[8,384]{1,0:T(8,128)}) custom-call(f32[1,4]{1,0:T(1,128)} %pw.1, s32[4,8]{1,0:T(4,128)} %bitcast.6, s32[1,1]{1,0:T(1,128)S(6)} %copy.15.cnt, bf16[4,8,8,384]{3,2,1,0:T(8,128)(2,1)} %bitcast.4, bf16[4,8,8,384]{3,2,1,0:T(8,128)(2,1)} %bitcast.5, f32[1,384]{1,0:T(1,128)} %cot_in.1, ...), custom_call_target="tpu_custom_call" | custom-call | tf_op jit(solution)/shard_map/main/pallas_call | solution.py:572
  46.9 1.7 %finish.1 = (f32[1,384]{1,0:T(1,128)}, bf16[4,8,8,384]{3,2,1,0:T(8,128)(2,1)}, f32[24,384]{1,0:T(8,128)}, f32[7,7,384]{2,1,0:T(8,128)}) custom-call(bf16[4,8,8,384]{3,2,1,0:T(8,128)(2,1)} %get-tuple-element.11.out, bf16[16,8,384]{2,1,0:T(8,128)(2,1)} %get-tuple-element.12.got4_in, f32[8,384]{1,0:T(8,128)} %get-tuple-element.13.emb_in), custom_call_target="tpu_custom_call" | custom-call | tf_op jit(solution)/shard_map/finish/pallas_call | solution.py:651
